TPU v7x, 32 devices: a whole 2x2x4 slice. The times are simulated.
32 devices in a mesh: lat: 4 (over z), lon: 4 (over y, x), rad: 2 (over core).
Axes of the slice: x: 2, y: 2, z: 4, core: 2. Of those that a mesh axis runs over, the one named last changes fastest.
Arguments:
- velocity: float32 [3, 32, 32, 1024], P(None, 'rad', 'lat', 'lon'), may hold values from -6 to 6
- forcing: float32 [3, 32, 32, 1024], P(None, 'rad', 'lat', 'lon'), may hold values from -6 to 6
- viscosity: float32 [32, 32, 1024], P('rad', 'lat', 'lon'), may hold values from 0.1 to 10
- plate_ids: int32 [4, 128], P('lat', 'lon'), may hold values from 0 to 11, as said below
Outputs:
- new_velocity: float32 [3, 32, 32, 1024], P(None, 'rad', 'lat', 'lon')
- coarse_residual: float32 [3, 16, 16, 512], P(None, None, 'lat', 'lon')
- plate_velocity: float32 [3, 32, 1024], P(None, 'lat', 'lon')
Inputs may be any that keep to these rules, and one draw needn't show every extreme that they name: `plate_ids`: every plate number from 0 to 11 names at least one face block.
All inputs are finite; a program needn't handle non-finite values.
Results may differ from a plain program's by a relative error of at most 0.0003.
Values sent between devices are 32-bit elements; how exact they have to be, the bound alone decides.
A program may use at most 64 MiB of HBM per device.

v0:
```python
import functools
import math

import jax
import jax.numpy as jnp
from jax import lax
from jax.experimental import pallas as pl
from jax.experimental.pallas import tpu as pltpu
from jax.sharding import PartitionSpec as P

SWEEPS = 3
PLATES = 12
FACE = 8
RELAX = 0.8
COMPS = 3
LANES = 128
SLOT = 32
MESH = pl.DeviceIdType.MESH
HIGHEST = lax.Precision.HIGHEST
UNROLL = 4


def harmonic(own, other):
    return 2.0 * own * other / (own + other)


class Link:
    def __init__(self, make):
        self.make = make

    def start(self):
        self.make().start()

    def wait_send(self):
        self.make().wait_send()

    def wait_recv(self):
        self.make().wait_recv()


def kernel(
    sizes, vel, forc, visc, ids_in,
    last, coarse, plate,
    early, ids, f, eta, w_lat, w_lon, w_rad, gain, diag,
    face_out, face_in, col_out, col_in, pairs,
    lat_sums, lon_sums, stage_out,
    load_sem, send_sem, recv_sem, s1_send, s1_recv, s2_send, s2_recv, g_send, g_recv,
):
    n_lat, n_lon, n_rad = sizes
    n_r, n_a, n_o = visc.shape
    me_lat, me_lon, me_rad = (lax.axis_index(a) for a in ("lat", "lon", "rad"))
    lat_lo, lat_hi = me_lat > 0, me_lat < n_lat - 1
    rad_lo, rad_hi = me_rad > 0, me_rad < n_rad - 1
    lon_up, lon_dn = lax.rem(me_lon + 1, n_lon), lax.rem(me_lon + n_lon - 1, n_lon)
    is_top = me_rad == n_rad - 1
    v = [early.at[t] for t in range(SWEEPS)] + [last]

    barrier = pltpu.get_barrier_semaphore()

    def greet(device):
        pl.semaphore_signal(barrier, inc=1, device_id=device, device_id_type=MESH)

    expected = 2
    greet({"lon": lon_up})
    greet({"lon": lon_dn})
    for has, device in (
        (lat_lo, {"lat": me_lat - 1}), (lat_hi, {"lat": me_lat + 1}),
        (rad_lo, {"rad": me_rad - 1}), (rad_hi, {"rad": me_rad + 1}),
    ):
        pl.when(has)(functools.partial(greet, device))
        expected = expected + jnp.where(has, 1, 0)
    if n_lat - 1 > SWEEPS + 1:
        for step in range(1, n_lat):
            greet({"lat": lax.rem(me_lat + step, n_lat)})
        expected = expected + (n_lat - 1)
    if n_lon // 2 + n_rad - 1 > SWEEPS + 1:
        for step in range(1, n_lon * n_rad):
            greet({
                "lon": lax.rem(me_lon + step // n_rad, n_lon),
                "rad": lax.rem(me_rad + step % n_rad, n_rad),
            })
        expected = expected + (n_lon * n_rad - 1)

    loads = [
        pltpu.make_async_copy(visc, eta.at[pl.ds(1, n_r)], load_sem.at[0]),
        pltpu.make_async_copy(vel, v[0].at[:, pl.ds(1, n_r)], load_sem.at[1]),
        pltpu.make_async_copy(forc, f, load_sem.at[2]),
        pltpu.make_async_copy(ids_in, ids, load_sem.at[3]),
    ]
    for load in loads:
        load.start()

    lane_wide = lax.broadcasted_iota(jnp.int32, (n_a, n_o), 1)
    lane = lax.broadcasted_iota(jnp.int32, (n_a, LANES), 1)
    row = lax.broadcasted_iota(jnp.int32, (n_a, n_o), 0)
    reps = n_o // LANES

    zero_plane = jnp.zeros((n_a, n_o), jnp.float32)
    for has, slot in ((rad_lo, 0), (rad_hi, n_r + 1)):
        @pl.when(jnp.logical_not(has))
        def _():
            eta[slot] = zero_plane
            for t in range(SWEEPS + 1):
                for c in range(COMPS):
                    v[t][c, slot] = zero_plane
    for has, side in ((lat_lo, 0), (lat_hi, 1)):
        @pl.when(jnp.logical_not(has))
        def _():
            for t in range(SWEEPS + 1):
                face_in[t, side] = jnp.zeros(face_in.shape[2:], jnp.float32)

    blocks_r = n_r // UNROLL
    order = [blocks_r - 1] + list(range(blocks_r - 1))

    def chunk(t, b):
        comps = COMPS + 1 if t == 0 else COMPS
        rows = pl.ds(b * UNROLL * comps, UNROLL * comps)

        def remote(src, dst, k, device):
            return Link(functools.partial(
                pltpu.make_async_remote_copy,
                src, dst, send_sem.at[t, b, k], recv_sem.at[t, b, k],
                device_id=device, device_id_type=MESH,
            ))

        sends = [
            (remote(col_out.at[t, b, 1], col_in.at[t, b, 0], 2, {"lon": lon_up}), None),
            (remote(col_out.at[t, b, 0], col_in.at[t, b, 1], 3, {"lon": lon_dn}), None),
            (remote(face_out.at[t, 1, rows], face_in.at[t, 0, rows], 0, {"lat": me_lat + 1}), lat_hi),
            (remote(face_out.at[t, 0, rows], face_in.at[t, 1, rows], 1, {"lat": me_lat - 1}), lat_lo),
        ]
        takes = [None, None, lat_lo, lat_hi]
        ups = [(remote(v[t].at[:, n_r], v[t].at[:, 0], 4, {"rad": me_rad + 1}), rad_hi)]
        downs = [(remote(v[t].at[:, 1], v[t].at[:, n_r + 1], 5, {"rad": me_rad - 1}), rad_lo)]
        if t == 0:
            ups.append((remote(eta.at[n_r], eta.at[0], 6, {"rad": me_rad + 1}), rad_hi))
            downs.append((remote(eta.at[1], eta.at[n_r + 1], 7, {"rad": me_rad - 1}), rad_lo))
        return sends, takes, ups, downs

    def guarded(cond, call):
        if cond is None:
            call()
        else:
            pl.when(cond)(call)

    def start(t, b):
        sends, _, _, _ = chunk(t, b)
        for copy, cond in sends:
            guarded(cond, copy.start)
        if b == blocks_r - 1:
            for copy, cond in chunk(t, 0)[2]:
                guarded(cond, copy.start)
        if b == 0:
            for copy, cond in chunk(t, 0)[3]:
                guarded(cond, copy.start)

    def arrive(t, b):
        sends, takes, _, _ = chunk(t, b)
        _, _, ups, downs = chunk(t, 0)
        if b == 0:
            for copy, _ in ups:
                guarded(rad_lo, copy.wait_recv)
        if b == blocks_r - 1:
            for copy, _ in downs:
                guarded(rad_hi, copy.wait_recv)
        for (copy, _), cond in zip(sends, takes):
            guarded(cond, copy.wait_recv)

    def sent(t):
        for b in range(blocks_r):
            for copy, cond in chunk(t, b)[0]:
                guarded(cond, copy.wait_send)
        _, _, ups, downs = chunk(t, 0)
        for copy, cond in ups + downs:
            guarded(cond, copy.wait_send)

    def lane_of(t, j, c):
        return j * (COMPS + 1 if t == 0 else COMPS) + c

    def row_of(t, r, c):
        return r * (COMPS + 1 if t == 0 else COMPS) + c

    def pack(t, b, j, c, tile, cols):
        face_out[t, 0, row_of(t, b * UNROLL + j, c)] = tile[:1]
        face_out[t, 1, row_of(t, b * UNROLL + j, c)] = tile[n_a - 1 :]
        k = lane_of(t, j, c)
        low, high = cols
        hit = lane == k
        low = jnp.where(hit, pltpu.roll(tile[:, :LANES], k, 1) if k else tile[:, :LANES], low)
        high = jnp.where(hit, pltpu.roll(tile[:, n_o - LANES :], (k + 1) % LANES, 1), high)
        return low, high

    def put_cols(t, b, cols):
        col_out[t, b, 0], col_out[t, b, 1] = cols

    no_cols = (jnp.zeros((n_a, LANES), jnp.float32),) * 2

    def shifted(t, b, j, c, tile, cols):
        col_lo, col_hi = cols
        k = lane_of(t, j, c)
        at = row_of(t, b * UNROLL + j, c)
        below = jnp.where(row == 0, face_in[t, 0, at], pltpu.roll(tile, 1, 0))
        above = jnp.where(row == n_a - 1, face_in[t, 1, at], pltpu.roll(tile, n_a - 1, 0))
        from_lo = pltpu.roll(col_lo, LANES - k, 1) if k else col_lo
        from_hi = pltpu.roll(col_hi, LANES - 1 - k, 1)
        west = jnp.where(lane_wide == 0, jnp.concatenate([from_lo] * reps, 1), pltpu.roll(tile, 1, 1))
        east = jnp.where(
            lane_wide == n_o - 1, jnp.concatenate([from_hi] * reps, 1), pltpu.roll(tile, n_o - 1, 1)
        )
        return below, above, west, east

    loads[0].wait()
    loads[1].wait()
    for b in order:
        cols = no_cols
        for j in range(UNROLL):
            r = b * UNROLL + j
            for c in range(COMPS):
                cols = pack(0, b, j, c, v[0][c, r + 1], cols)
            cols = pack(0, b, j, COMPS, eta[r + 1], cols)
        put_cols(0, b, cols)
    pl.semaphore_wait(barrier, expected)
    for b in order:
        start(0, b)

    loads[3].wait()
    lat_cell = (me_lat * n_a + row).astype(jnp.float32)
    lon_cell = (me_lon * n_o + lane_wide).astype(jnp.float32)
    phi = math.pi * ((lat_cell + 0.5) / (n_lat * n_a) - 0.5)
    lam = (2.0 * math.pi) * (lon_cell[:1] + 0.5) / (n_lon * n_o)
    cos_lat = jnp.cos(phi)
    rx = cos_lat * jnp.cos(lam)
    ry = cos_lat * jnp.sin(lam)
    rz = jnp.sin(phi)
    blocks = ids.shape[1]
    spread_rows = lax.broadcasted_iota(jnp.int32, (blocks, n_o), 0)
    spread_cols = lax.broadcasted_iota(jnp.int32, (blocks, n_o), 1)
    spread = (spread_cols // FACE == spread_rows).astype(jnp.float32)
    numbers = lax.broadcasted_iota(jnp.int32, (SLOT, n_o), 0)
    onehots = []
    for band in range(n_a // FACE):
        own = jnp.broadcast_to(ids[band : band + 1].astype(jnp.float32), (8, blocks))
        cells = jnp.dot(own, spread, precision=HIGHEST)[:1]
        onehots.append((jnp.abs(cells - numbers.astype(jnp.float32)) < 0.5).astype(jnp.float32))

    def weigh(b, cols):
        for j in range(UNROLL):
            r = b * UNROLL + j
            own = eta[r + 1]
            near = shifted(0, b, j, COMPS, own, cols)
            below, above, west, east = (harmonic(own, other) for other in near)
            down = harmonic(own, eta[r]) if j == 0 else up
            up = harmonic(own, eta[r + 2])
            w_lat[0, r] = below
            w_lat[1, r] = above
            w_lon[0, r] = west
            w_lon[1, r] = east
            w_rad[r] = down
            w_rad[r + 1] = up
            d = 0.5 * own + (below + above) + (west + east) + (up + down)
            diag[r] = d
            gain[r] = RELAX / d

    def flux(t, b, j, c, cols):
        r = b * UNROLL + j
        tile = v[t][c, r + 1]
        below, above, west, east = shifted(t, b, j, c, tile, cols)
        total = (
            (w_lat[0, r] * below + w_lat[1, r] * above)
            + (w_lon[0, r] * west + w_lon[1, r] * east)
            + (w_rad[r] * v[t][c, r] + w_rad[r + 1] * v[t][c, r + 2])
        )
        return tile, f[c, r] + total

    def s1_copy(step):
        return pltpu.make_async_remote_copy(
            stage_out.at[0], lat_sums.at[me_lat], s1_send.at[step - 1], s1_recv.at[me_lat],
            device_id={"lat": lax.rem(me_lat + step, n_lat)}, device_id_type=MESH,
        )

    def s2_copy(step):
        return pltpu.make_async_remote_copy(
            stage_out.at[1], lon_sums.at[me_lon], s2_send.at[step - 1], s2_recv.at[me_lon],
            device_id={
                "lon": lax.rem(me_lon + step // n_rad, n_lon),
                "rad": lax.rem(me_rad + step % n_rad, n_rad),
            },
            device_id_type=MESH,
        )

    def received(buffer, sem, index):
        pltpu.make_async_remote_copy(
            stage_out.at[0], buffer.at[index], s1_send.at[0], sem.at[index],
            device_id={"lon": lon_up}, device_id_type=MESH,
        ).wait_recv()

    def torques():
        drag = [eta[n_r] * (last[c, n_r] - last[c, n_r - 1]) for c in range(COMPS)]
        twist = (
            (ry * drag[2] - rz * drag[1]) * cos_lat,
            (rz * drag[0] - rx * drag[2]) * cos_lat,
            (rx * drag[1] - ry * drag[0]) * cos_lat,
            cos_lat,
        )
        packed = jnp.zeros((1, LANES), jnp.float32)
        for band in range(n_a // FACE):
            cut = slice(band * FACE, (band + 1) * FACE)
            rows = jnp.concatenate(
                [jnp.sum(x[cut], axis=0, keepdims=True) for x in twist]
                + [jnp.zeros((4, n_o), jnp.float32)], 0,
            )
            sums = lax.dot_general(
                rows, onehots[band], (((1,), (1,)), ((), ())), precision=HIGHEST,
                preferred_element_type=jnp.float32,
            )
            packed = packed + jnp.concatenate([sums[i : i + 1] for i in range(COMPS + 1)], 1)
        stage_out[0] = packed
        lat_sums[me_lat] = packed
        for step in range(1, n_lat):
            s1_copy(step).start()

    for t in range(SWEEPS):
        for b in order:
            arrive(t, b)
            cols_in = (col_in[t, b, 0], col_in[t, b, 1])
            if t == 0:
                weigh(b, cols_in)
                if b == order[0]:
                    loads[2].wait()
            cols = no_cols
            for j in range(UNROLL):
                r = b * UNROLL + j
                for c in range(COMPS):
                    tile, total = flux(t, b, j, c, cols_in)
                    fresh = (1.0 - RELAX) * tile + gain[r] * total
                    v[t + 1][c, r + 1] = fresh
            for j in range(UNROLL):
                for c in range(COMPS):
                    cols = pack(t + 1, b, j, c, v[t + 1][c, b * UNROLL + j + 1], cols)
            put_cols(t + 1, b, cols)
            if t == SWEEPS - 1 and b == blocks_r - 1:
                pl.when(is_top)(torques)
            start(t + 1, b)

    @pl.when(is_top)
    def _():
        for step in range(1, n_lat):
            received(lat_sums, s1_recv, lax.rem(me_lat + step, n_lat))
        total = lat_sums[0]
        for i in range(1, n_lat):
            total = total + lat_sums[i]
        stage_out[1] = total
        lon_sums[me_lon] = total
        for step in range(1, n_lon * n_rad):
            s2_copy(step).start()

    for b in order:
        arrive(SWEEPS, b)
        cols_in = (col_in[SWEEPS, b, 0], col_in[SWEEPS, b, 1])
        for i in range(UNROLL // 2):
            for c in range(COMPS):
                two = jnp.zeros((n_a, n_o), jnp.float32)
                for j in (2 * i, 2 * i + 1):
                    tile, total = flux(SWEEPS, b, j, c, cols_in)
                    two = two + (total - diag[b * UNROLL + j] * tile)
                at = pl.ds((c * (n_r // 2) + b * (UNROLL // 2) + i) * n_a, n_a)
                for h in range(reps):
                    pairs[h, at] = two[:, h * LANES : (h + 1) * LANES]
    half = n_o // 2
    thin_r = lax.broadcasted_iota(jnp.int32, (LANES, half), 0)
    thin_c = lax.broadcasted_iota(jnp.int32, (LANES, half), 1)
    count = COMPS * (n_r // 2) * n_a // 2
    merged = jnp.zeros((count, half), jnp.float32)
    for h in range(reps):
        pick = jnp.where((thin_r + h * LANES) // 2 == thin_c, 0.125, 0.0).astype(jnp.bfloat16)
        both = pairs[h, pl.ds(0, count, stride=2)] + pairs[h, pl.ds(1, count, stride=2)]
        big = both.astype(jnp.bfloat16)
        small = (both - big.astype(jnp.float32)).astype(jnp.bfloat16)
        merged = merged + (
            jnp.dot(big, pick, preferred_element_type=jnp.float32)
            + jnp.dot(small, pick, preferred_element_type=jnp.float32)
        )
    mine = count // COMPS
    spot = pl.ds(pl.multiple_of(me_rad * mine, mine), mine)
    for c in range(COMPS):
        coarse[c, spot] = merged[c * mine : (c + 1) * mine]

    def g_copy(step):
        return pltpu.make_async_remote_copy(
            coarse.at[:, spot], coarse.at[:, spot], g_send.at[step - 1], g_recv.at[me_rad],
            device_id={"rad": lax.rem(me_rad + step, n_rad)}, device_id_type=MESH,
        )

    for step in range(1, n_rad):
        g_copy(step).start()

    for i in range(n_lon):
        @pl.when(jnp.logical_or(jnp.logical_not(is_top), me_lon != i))
        def _():
            received(lon_sums, s2_recv, i)
    total = lon_sums[0]
    for i in range(1, n_lon):
        total = total + lon_sums[i]
    area = total[:, COMPS * SLOT : (COMPS + 1) * SLOT]
    valid = lax.broadcasted_iota(jnp.int32, (1, SLOT), 1) < PLATES
    root = jnp.sqrt(jnp.where(valid, area, 1.0))
    turns = jnp.concatenate(
        [total[:, i * SLOT : (i + 1) * SLOT] / root for i in range(COMPS)]
        + [jnp.zeros((8 - COMPS, SLOT), jnp.float32)], 0,
    )
    for band in range(n_a // FACE):
        cut = slice(band * FACE, (band + 1) * FACE)
        cell = jnp.dot(turns, onehots[band], precision=HIGHEST, preferred_element_type=jnp.float32)
        ox, oy, oz = (cell[i : i + 1] for i in range(COMPS))
        plate[0, cut] = oy * rz[cut] - oz * ry[cut]
        plate[1, cut] = oz * rx[cut] - ox * rz[cut]
        plate[2, cut] = ox * ry[cut] - oy * rx[cut]

    for t in range(SWEEPS + 1):
        sent(t)

    @pl.when(is_top)
    def _():
        for step in range(1, n_lat):
            s1_copy(step).wait_send()
        for step in range(1, n_lon * n_rad):
            s2_copy(step).wait_send()

    for step in range(1, n_rad):
        source = lax.rem(me_rad + step, n_rad)
        region = coarse.at[:, pl.ds(pl.multiple_of(source * mine, mine), mine)]
        pltpu.make_async_remote_copy(
            region, region, g_send.at[0], g_recv.at[source],
            device_id={"rad": source}, device_id_type=MESH,
        ).wait_recv()
        g_copy(step).wait_send()


def write_out(last, coarse, plate, new_v_out, coarse_out, plate_out, sem):
    n_r = new_v_out.shape[1]
    copies = [
        pltpu.make_async_copy(last.at[:, pl.ds(1, n_r)], new_v_out, sem.at[0]),
        pltpu.make_async_copy(coarse, coarse_out, sem.at[1]),
        pltpu.make_async_copy(plate, plate_out, sem.at[2]),
    ]
    for copy in copies:
        copy.start()
    for copy in copies:
        copy.wait()


def on_device(sizes, velocity, forcing, viscosity, plate_ids):
    n_lat, n_lon, n_rad = sizes
    _, n_r, n_a, n_o = velocity.shape
    rounds = SWEEPS + 1
    chunks = n_r // UNROLL
    f32 = jnp.float32
    dma = pltpu.SemaphoreType.DMA
    in_any = pl.BlockSpec(memory_space=pl.ANY)
    in_vmem = pl.BlockSpec(memory_space=pltpu.VMEM)
    coarse_rows = n_rad * (n_r // 2) * (n_a // 2)
    held = pl.pallas_call(
        functools.partial(kernel, sizes),
        out_shape=(
            pltpu.VMEM((COMPS, n_r + 2, n_a, n_o), f32),
            pltpu.VMEM((COMPS, coarse_rows, n_o // 2), f32),
            pltpu.VMEM((COMPS, n_a, n_o), f32),
        ),
        in_specs=[pl.BlockSpec(memory_space=pltpu.HBM)] * 4,
        out_specs=(in_vmem,) * 3,
        scratch_shapes=[
            pltpu.VMEM((SWEEPS, COMPS, n_r + 2, n_a, n_o), f32),
            pltpu.VMEM(plate_ids.shape, jnp.int32),
            pltpu.VMEM((COMPS, n_r, n_a, n_o), f32),
            pltpu.VMEM((n_r + 2, n_a, n_o), f32),
            pltpu.VMEM((2, n_r, n_a, n_o), f32),
            pltpu.VMEM((2, n_r, n_a, n_o), f32),
            pltpu.VMEM((n_r + 1, n_a, n_o), f32),
            pltpu.VMEM((n_r, n_a, n_o), f32),
            pltpu.VMEM((n_r, n_a, n_o), f32),
            pltpu.VMEM((rounds, 2, (COMPS + 1) * n_r, 1, n_o), f32),
            pltpu.VMEM((rounds, 2, (COMPS + 1) * n_r, 1, n_o), f32),
            pltpu.VMEM((rounds, chunks, 2, n_a, LANES), f32),
            pltpu.VMEM((rounds, chunks, 2, n_a, LANES), f32),
            pltpu.VMEM((n_o // LANES, COMPS * (n_r // 2) * n_a, LANES), f32),
            pltpu.VMEM((n_lat, 1, LANES), f32),
            pltpu.VMEM((n_lon, 1, LANES), f32),
            pltpu.VMEM((2, 1, LANES), f32),
            dma((4,)),
            dma((rounds, chunks, 8)),
            dma((rounds, chunks, 8)),
            dma((n_lat,)),
            dma((n_lat,)),
            dma((n_lon * n_rad,)),
            dma((n_lon,)),
            dma((n_rad,)),
            dma((n_rad,)),
        ],
        compiler_params=pltpu.CompilerParams(
            collective_id=0, has_side_effects=True, vmem_limit_bytes=24 * 2**20
        ),
    )(*(
        pltpu.with_memory_space_constraint(x, pltpu.HBM)
        for x in (velocity, forcing, viscosity, plate_ids)
    ))
    new_v, coarse, plate = pl.pallas_call(
        write_out,
        out_shape=(
            jax.ShapeDtypeStruct(velocity.shape, f32),
            jax.ShapeDtypeStruct((COMPS, coarse_rows, n_o // 2), f32),
            jax.ShapeDtypeStruct((COMPS, n_a, n_o), f32),
        ),
        in_specs=[in_vmem] * 3,
        out_specs=(in_any,) * 3,
        scratch_shapes=[dma((3,))],
        compiler_params=pltpu.CompilerParams(vmem_limit_bytes=4 * 2**20),
    )(*(pltpu.with_memory_space_constraint(x, pltpu.VMEM) for x in held))
    coarse = coarse.reshape(COMPS, n_rad * (n_r // 2), n_a // 2, n_o // 2)
    return new_v, coarse, plate


def solution(mesh):
    sizes = tuple(mesh.shape[a] for a in ("lat", "lon", "rad"))
    field = P(None, "rad", "lat", "lon")
    return jax.shard_map(
        functools.partial(on_device, sizes),
        mesh=mesh,
        in_specs=(field, field, P("rad", "lat", "lon"), P("lat", "lon")),
        out_specs=(field, P(None, None, "lat", "lon"), P(None, "lat", "lon")),
        check_vma=False,
    )
```

profile of v0, /device:TPU:0, one launch (start us, length us, event | category | flops | bytes accessed | tf_op | source)
XLA Modules:
  0.0 23.5 jit_solution(13255771770570919089)
XLA Ops:
  0.6 22.0 %shard_map.67 = (f32[3,18,8,256]{3,2,1,0:T(8,128)S(1)}, f32[3,64,128]{2,1,0:T(8,128)S(1)}, f32[3,8,256]{2,1,0:T(8,128)S(1)}) custom-call(f32[3,16,8,256]{3,2,1,0:T(8,128)} %vel.1, f32[3,16,8,256]{3,2,1,0:T(8,128)} %forc.1, f32[16,8,256]{2,1,0:T(8,128)} %visc.1, s32[1,32]{1,0:T(1,128)} %ids_in.1), custom_call_target="tpu_custom_call" | custom-call | tf_op jit(solution)/shard_map/pallas_call | solution.py:462
  22.7 0.8 %shard_map.68 = (f32[3,16,8,256]{3,2,1,0:T(8,128)}, f32[3,64,128]{2,1,0:T(8,128)}, f32[3,8,256]{2,1,0:T(8,128)}) custom-call(f32[3,18,8,256]{3,2,1,0:T(8,128)S(1)} %get-tuple-element.9.last, f32[3,64,128]{2,1,0:T(8,128)S(1)} %get-tuple-element.10.coarse, f32[3,8,256]{2,1,0:T(8,128)S(1)} %get-tuple-element.11.plate), custom_call_target="tpu_custom_call" | custom-call | tf_op jit(solution)/shard_map/pallas_call | solution.py:506
where the time goes:
time: 23.6 us; the launch traced here: 23.5 us
  Pallas kernels  22.8 us (97%)
  between operations  0.64 us (3%)
    pallas_call x1, Pallas kernels, on_device(): pl.pallas_call(functools.partial(kernel, sizes), out_shape=(pltpu.VMEM((C...  22 us
    pallas_call x1, Pallas kernels, on_device(): pl.pallas_call(write_out, out_shape=(jax.ShapeDtypeStruct(velocity.shape,...  0.8 us

commit v1 on v0

v1 whole, which is shorter than its diff:
```python
import functools
import math

import jax
import jax.numpy as jnp
from jax import lax
from jax.experimental import pallas as pl
from jax.experimental.pallas import tpu as pltpu
from jax.sharding import PartitionSpec as P

SWEEPS = 3
PLATES = 12
FACE = 8
RELAX = 0.8
COMPS = 3
LANES = 128
SLOT = 32
MESH = pl.DeviceIdType.MESH
HIGHEST = lax.Precision.HIGHEST
UNROLL = 4
DIRECT = 64
FIELDS = 2 * (COMPS + 1)


def harmonic(own, other):
    return 2.0 * own * other / (own + other)


def harmonic0(own, other):
    return 2.0 * own * other / jnp.maximum(own + other, 1e-30)


class Link:
    def __init__(self, make):
        self.make = make

    def start(self):
        self.make().start()

    def wait_send(self):
        self.make().wait_send()

    def wait_recv(self):
        self.make().wait_recv()


def kernel(
    sizes, vel, forc, visc, ids_in,
    last, coarse, plate,
    early, ids, ids_near, f, eta, w_lat, w_lon, w_rad, gain, diag, part, num,
    row_out, row_in, row_sum, row_w, row_g, row_q, row_p,
    col_out, col_in, col_sum, col_w, col_g, col_d, col_p,
    plane_num, plane_d, plane_g, plane_l, plane_q,
    corner_out, corner_in, corner_t, edge_in, side_in,
    pairs, sums, lat_sums, stage_out, tally, tally_thin,
    load_sem, lon_send, lat_send, rad_send, edge_send, lon_recv, lat_recv, rad_recv, edge_recv,
    ids_send, ids_recv, wave, s1_send, s1_recv, s2_send, s2_recv, g_send, g_recv,
):
    n_lat, n_lon, n_rad = sizes
    n_r, n_a, n_o = visc.shape
    me_lat, me_lon, me_rad = (lax.axis_index(a) for a in ("lat", "lon", "rad"))
    lat_has = (me_lat > 0, me_lat < n_lat - 1)
    rad_has = (me_rad > 0, me_rad < n_rad - 1)
    lat_to = (me_lat - 1, me_lat + 1)
    rad_to = (me_rad - 1, me_rad + 1)
    lon_to = (lax.rem(me_lon + n_lon - 1, n_lon), lax.rem(me_lon + 1, n_lon))
    is_top = me_rad == n_rad - 1
    direct = n_lat * n_lon * n_rad <= DIRECT
    v = [early.at[t] for t in range(SWEEPS)] + [last]
    blocks_r = n_r // UNROLL
    end = blocks_r - 1
    both = (0, 1)

    def guarded(cond, call):
        if cond is None:
            call()
        else:
            pl.when(cond)(call)

    def all_of(*conds):
        conds = [c for c in conds if c is not None]
        return functools.reduce(jnp.logical_and, conds)

    barrier = pltpu.get_barrier_semaphore()

    def greet(device):
        pl.semaphore_signal(barrier, inc=1, device_id=device, device_id_type=MESH)

    expected = n_lon * n_rad - 1
    for step in range(1, n_lon * n_rad):
        greet({
            "lon": lax.rem(me_lon + step // n_rad, n_lon),
            "rad": lax.rem(me_rad + step % n_rad, n_rad),
        })
    for s in both:
        if direct:
            pl.when(lat_has[s])(functools.partial(greet, {"lat": lat_to[s]}))
            expected = expected + jnp.where(lat_has[s], 1, 0)
        for q in both:
            pl.when(lat_has[s])(functools.partial(greet, {"lat": lat_to[s], "lon": lon_to[q]}))
            expected = expected + jnp.where(lat_has[s], 1, 0)
        for p in both:
            has = all_of(lat_has[s], rad_has[p])
            pl.when(has)(functools.partial(greet, {"lat": lat_to[s], "rad": rad_to[p]}))
            expected = expected + jnp.where(has, 1, 0)
    if not direct:
        for step in range(1, n_lat):
            greet({"lat": lax.rem(me_lat + step, n_lat)})
        expected = expected + (n_lat - 1)

    def load_chunk(b):
        here_r = pl.ds(b * UNROLL, UNROLL)
        inner = pl.ds(1 + b * UNROLL, UNROLL)
        return [
            pltpu.make_async_copy(visc.at[here_r], eta.at[inner], load_sem.at[b]),
            pltpu.make_async_copy(vel.at[:, here_r], v[0].at[:, inner], load_sem.at[b]),
            pltpu.make_async_copy(forc.at[:, here_r], f.at[:, here_r], load_sem.at[b]),
        ]

    for b in reversed(range(blocks_r)):
        for load in load_chunk(b):
            load.start()
    load_ids = pltpu.make_async_copy(ids_in, ids, load_sem.at[blocks_r])
    load_ids.start()

    def rows_of(ref):
        return ref.size // n_o

    def await_rows(sem, rows, sending=False):
        some = tally.at[pl.ds(0, rows)]
        copy = pltpu.make_async_remote_copy(
            some, some, sem, sem, device_id={"lon": lon_to[1]}, device_id_type=MESH,
        )
        copy.wait_send() if sending else copy.wait_recv()

    def await_thin(sem, rows, sending=False):
        some = tally_thin.at[pl.ds(0, rows)]
        copy = pltpu.make_async_remote_copy(
            some, some, sem, sem, device_id={"lon": lon_to[1]}, device_id_type=MESH,
        )
        copy.wait_send() if sending else copy.wait_recv()

    def loaded(b):
        some = tally.at[pl.ds(0, (2 * COMPS + 1) * UNROLL * n_a)]
        pltpu.make_async_copy(some, some, load_sem.at[b]).wait()

    lane_wide = lax.broadcasted_iota(jnp.int32, (n_a, n_o), 1)
    lane = lax.broadcasted_iota(jnp.int32, (n_a, LANES), 1)
    row = lax.broadcasted_iota(jnp.int32, (n_a, n_o), 0)
    row_thin = lax.broadcasted_iota(jnp.int32, (n_a, LANES), 0)
    even = lane % 2 == 0
    field_of = (lane + 1) % LANES // 2 % FIELDS
    layer_of = (lane + 1) % LANES // (2 * FIELDS)
    reps = n_o // LANES
    row_edge = (0, n_a - 1)
    lane_edge = (0, n_o - 1)
    thin_edge = (0, LANES - 1)

    plane_rows = n_a
    tile_rows = n_a * LANES // n_o

    def phase(call):
        pl.when(me_lat >= 0)(call)

    for p, slot, face in ((0, 0, 0), (1, n_r + 1, n_r)):
        @pl.when(jnp.logical_not(rad_has[p]))
        def _():
            zero_plane = jnp.zeros((n_a, n_o), jnp.float32)
            w_rad[face] = zero_plane
            for t in range(SWEEPS + 1):
                for c in range(COMPS):
                    v[t][c, slot] = zero_plane
            for h in both:
                for s in both:
                    edge_in[h, s, p] = zero_plane
                    side_in[h, p, s] = jnp.zeros((n_a, LANES), jnp.float32)
    for s in both:
        @pl.when(jnp.logical_not(lat_has[s]))
        def _():
            blank_rows = jnp.where(row == FIELDS - 1, 1.0, 0.0)
            for h in both:
                for r in range(n_r):
                    row_in[h, s, r] = blank_rows
                for b in range(blocks_r):
                    for q in both:
                        corner_in[h, b, s, q] = jnp.zeros((1, LANES), jnp.float32)
                for p in both:
                    edge_in[h, s, p] = jnp.zeros((n_a, n_o), jnp.float32)
            ids_near[s] = jnp.zeros(ids.shape, jnp.int32)

    def messages(h, b):
        t = 2 * h
        table = []

        def add(src, dst, sends, takes, device, cond):
            table.append((Link(functools.partial(
                pltpu.make_async_remote_copy, src, dst, sends, takes,
                device_id=device, device_id_type=MESH,
            )), cond))

        for p, layer, slot in ((0, 1, n_r + 1), (1, n_r, 0)):
            if p not in near_planes(b):
                continue
            sems = (rad_send.at[p], rad_recv.at[h, 1 - p])
            device = {"rad": rad_to[p]}
            add(v[t].at[:, layer], v[t].at[:, slot], *sems, device, rad_has[p])
            add(num.at[h, :, layer - 1], plane_num.at[h, 1 - p], *sems, device, rad_has[p])
            if h == 0:
                add(eta.at[layer], eta.at[slot], *sems, device, rad_has[p])
                add(part.at[layer - 1], plane_d.at[1 - p], *sems, device, rad_has[p])
            for q in both:
                add(
                    col_out.at[h, b], side_in.at[h, 1 - p, 1 - q], *sems,
                    {"lon": lon_to[q], "rad": rad_to[p]}, rad_has[p],
                )
            for s in both:
                add(
                    row_out.at[h, s, layer - 1], edge_in.at[h, 1 - s, 1 - p],
                    edge_send.at[s, p], edge_recv.at[h, 1 - s, 1 - p],
                    {"lat": lat_to[s], "rad": rad_to[p]}, all_of(rad_has[p], lat_has[s]),
                )
        for q in both:
            add(
                col_out.at[h, b], col_in.at[h, b, 1 - q], lon_send.at[0], lon_recv.at[h, b],
                {"lon": lon_to[q]}, None,
            )
        for s in both:
            for q in both:
                add(
                    corner_out.at[h, b, s], corner_in.at[h, b, 1 - s, 1 - q],
                    lat_send.at[s], lat_recv.at[h, b, 1 - s],
                    {"lat": lat_to[s], "lon": lon_to[q]}, lat_has[s],
                )
        layers = pl.ds(b * UNROLL, UNROLL)
        for s in both:
            add(
                row_out.at[h, s, layers], row_in.at[h, 1 - s, layers],
                lat_send.at[s], lat_recv.at[h, b, 1 - s], {"lat": lat_to[s]}, lat_has[s],
            )
        return table

    corner_rows = 2 * LANES // n_o
    lat_rows = UNROLL * FIELDS + corner_rows

    def rad_rows(h):
        return (2 * COMPS + (2 if h == 0 else 0)) * n_a + 2 * tile_rows

    def start(h, b):
        for copy, cond in messages(h, b):
            guarded(cond, copy.start)

    def near_planes(b):
        return [p for p, at in ((0, 0), (1, end)) if b == at]

    def arrive(h, b):
        for p in near_planes(b):
            guarded(rad_has[p], functools.partial(await_rows, rad_recv.at[h, p], rad_rows(h)))
            for s in both:
                guarded(
                    all_of(rad_has[p], lat_has[s]),
                    functools.partial(await_rows, edge_recv.at[h, s, p], FIELDS),
                )
        await_rows(lon_recv.at[h, b], 2 * tile_rows)
        for s in both:
            guarded(lat_has[s], functools.partial(await_rows, lat_recv.at[h, b, s], lat_rows))

    def sent(h):
        for p in both:
            guarded(rad_has[p], functools.partial(await_rows, rad_send.at[p], rad_rows(h), True))
            for s in both:
                guarded(
                    all_of(rad_has[p], lat_has[s]),
                    functools.partial(await_rows, edge_send.at[s, p], FIELDS, True),
                )
        await_rows(lon_send.at[0], blocks_r * 2 * tile_rows, True)
        for s in both:
            guarded(lat_has[s], functools.partial(await_rows, lat_send.at[s], blocks_r * lat_rows, True))

    def turn(x, shift, axis):
        shift = shift % x.shape[axis]
        return pltpu.roll(x, shift, axis) if shift else x

    def interior(t, r, c):
        tile = v[t][c, r + 1]
        return tile, (
            (w_lat[0, r] * turn(tile, 1, 0) + w_lat[1, r] * turn(tile, -1, 0))
            + (w_lon[0, r] * turn(tile, 1, 1) + w_lon[1, r] * turn(tile, -1, 1))
        )

    def radial(t, r, c, seams):
        total = None
        for face, slot in ((r, r), (r + 1, r + 2)):
            if (slot in (0, n_r + 1)) == seams or (seams is None):
                term = w_rad[face] * v[t][c, slot]
                total = term if total is None else total + term
        return total

    def lane_at(g, j):
        return 2 * (j * FIELDS + g)

    def ends_of(x, k):
        x = turn(x, -k, 1)
        west = jnp.where(lane == 0, x, 0.0)
        east = jnp.where(lane == LANES - 1, x, 0.0)
        if reps == 1:
            return west + east
        gap = [jnp.zeros((n_a, LANES), jnp.float32)] * (reps - 2)
        return jnp.concatenate([west] + gap + [east], 1)

    def edge_rows(low, high):
        return jnp.where(row == 0, low, jnp.where(row == n_a - 1, high, 0.0))

    def seams(t, b, j, c):
        r = b * UNROLL + j
        low, high = (row_sum[t, s, r, 1 + c : 2 + c] for s in both)
        return edge_rows(low, high) + ends_of(col_sum[t, b], lane_at(1 + c, j))

    def pack(h, r, k, tile, packed):
        row_out[h, 0, r, k : k + 1, :] = tile[:1]
        row_out[h, 1, r, k : k + 1, :] = tile[n_a - 1 :]
        at = lane_at(k, r % UNROLL)
        two = jnp.where(lane < LANES // 2, tile[:, :LANES], tile[:, n_o - LANES :])
        hit = jnp.logical_and(field_of == k, layer_of == r % UNROLL)
        return jnp.where(hit, turn(two, at, 1), packed)

    def prepare(h, b):
        t = 2 * h
        packed = jnp.zeros((n_a, LANES), jnp.float32)
        for j in range(UNROLL):
            r = b * UNROLL + j
            if h == 0:
                own = eta[r + 1]
                below = jnp.where(row == 0, 0.0, harmonic(own, turn(own, 1, 0)))
                above = jnp.where(row == n_a - 1, 0.0, turn(below, -1, 0))
                west = jnp.where(lane_wide == 0, 0.0, harmonic(own, turn(own, 1, 1)))
                east = jnp.where(lane_wide == n_o - 1, 0.0, turn(west, -1, 1))
                w_lat[0, r] = below
                w_lat[1, r] = above
                w_lon[0, r] = west
                w_lon[1, r] = east
                d = 0.5 * own + (below + above) + (west + east)
                if r > 0:
                    down = harmonic(own, eta[r])
                    w_rad[r] = down
                    d = d + down
                if r < n_r - 1:
                    d = d + harmonic(own, eta[r + 2])
                part[r] = d
                packed = pack(h, r, 0, own, packed)
                packed = pack(h, r, FIELDS - 1, d, packed)
        for j in range(UNROLL):
            r = b * UNROLL + j
            for c in range(COMPS):
                tile, near = interior(t, r, c)
                if h == 0:
                    total = f[c, r] + near
                    if r > 0:
                        total = total + w_rad[r] * v[t][c, r]
                    if r < n_r - 1:
                        up = w_rad[r + 1] if j < UNROLL - 1 else harmonic(eta[r + 1], eta[r + 2])
                        total = total + up * v[t][c, r + 2]
                else:
                    total = f[c, r] + (near + radial(t, r, c, False))
                num[h, c, r] = total
                packed = pack(h, r, 1 + c, tile, packed)
                packed = pack(h, r, 1 + COMPS + c, total, packed)
        col_out[h, b] = packed
        for s in both:
            corner_out[h, b, s] = packed[row_edge[s] : row_edge[s] + 1]

    def repeat_from(x, field, shifts):
        fields = field_of if x.shape[0] == n_a else field_of[:1]
        only = jnp.where(fields == field, x, 0.0)
        return functools.reduce(jnp.add, [turn(only, 2 * k, 1) for k in shifts])

    def repeat_first(x):
        return repeat_from(x, 0, range(COMPS + 1))

    def repeat_last(x):
        return repeat_from(x, FIELDS - 1, [1 + c - (FIELDS - 1) for c in range(COMPS)])

    def joined(from_west, from_east):
        at = even if from_west.shape[0] == n_a else even[:1]
        return jnp.where(at, turn(from_west, 1, 1), turn(from_east, -1, 1))

    def update_rows(h, b):
        t = 2 * h
        stacked = jnp.zeros((8, LANES), jnp.float32)
        spot = lax.broadcasted_iota(jnp.int32, (8, LANES), 0)
        for s in both:
            stacked = jnp.where(spot == 2 * s, turn(corner_in[h, b, s, 0], 1, 1), stacked)
            stacked = jnp.where(spot == 2 * s + 1, corner_in[h, b, s, 1], stacked)
        corner_t[h, b] = stacked.T
        for s in both:
            for j in range(UNROLL):
                r = b * UNROLL + j
                own, far = row_out[h, s, r], row_in[h, s, r]
                column = corner_t[h, b, pl.ds(lane_at(0, j), FIELDS, stride=2), :]
                west = jnp.where(lane == 0, column[:, 2 * s : 2 * s + 1], 0.0)
                east = jnp.where(lane == LANES - 1, column[:, 2 * s + 1 : 2 * s + 2], 0.0)
                if reps == 1:
                    corner = west + east
                else:
                    gap = [jnp.zeros((n_a, LANES), jnp.float32)] * (reps - 2)
                    corner = jnp.concatenate([west] + gap + [east], 1)
                near = [p for p, layer in ((0, 0), (1, n_r - 1)) if r == layer]
                if h == 0:
                    far_eta = far[:1]
                    w = harmonic(far_eta, own[:1])
                    wq = harmonic0(far_eta, corner[:1])
                    d = far[FIELDS - 1 :] + (w + wq)
                    for p in near:
                        wp = harmonic0(far_eta, edge_in[h, s, p, :1])
                        row_p[s, p] = wp
                        d = d + wp
                    row_w[s, r] = w
                    row_q[s, r] = wq
                    row_g[s, r] = RELAX / d
                w = row_w[s, r]
                total = turn(far, -COMPS, 0) + w * own + row_q[s, r] * corner
                for p in near:
                    total = total + row_p[s, p] * edge_in[h, s, p]
                row_sum[t, s, r] = w * far
                row_sum[t + 1, s, r] = w * ((1.0 - RELAX) * far + row_g[s, r] * total)

    def side_of(h, p):
        return joined(side_in[h, p, 0], side_in[h, p, 1])

    def update_cols(h, b):
        t = 2 * h
        far = joined(col_in[h, b, 0], col_in[h, b, 1])
        own = col_out[h, b]
        corners = [joined(corner_in[h, b, s, 0], corner_in[h, b, s, 1]) for s in both]
        move = 2 * FIELDS * (UNROLL - 1)
        sides = {p: turn(side_of(h, p), -move if p == 0 else move, 1) for p in near_planes(b)}
        if h == 0:
            far_eta = repeat_first(far)
            w = harmonic0(far_eta, repeat_first(own))
            d = repeat_last(far) + w
            for s in both:
                wd = jnp.where(
                    row_thin == row_edge[s], harmonic0(far_eta, repeat_first(corners[s])), 0.0,
                )
                col_d[b, s] = wd
                d = d + wd
            for p in near_planes(b):
                wp = jnp.where(
                    layer_of == (0, UNROLL - 1)[p], harmonic0(far_eta, repeat_first(sides[p])), 0.0,
                )
                col_p[p] = wp
                d = d + wp
            col_w[b] = w
            col_g[b] = RELAX / jnp.where(d > 0.0, d, 1.0)
        w = col_w[b]
        total = turn(far, -2 * COMPS, 1) + w * own
        for s in both:
            total = total + col_d[b, s] * corners[s]
        for p in near_planes(b):
            total = total + col_p[p] * sides[p]
        col_sum[t, b] = w * far
        col_sum[t + 1, b] = w * ((1.0 - RELAX) * far + col_g[b] * total)

    def update_plane(h, p):
        t = 2 * h
        slot, layer, face, j = ((0, 1, 0, UNROLL - 1), (n_r + 1, n_r, n_r, 0))[p]
        side = side_of(h, p)
        if h == 0:
            own = eta[slot]
            w = harmonic(own, eta[layer])
            w_rad[face] = w
            wq = harmonic0(own, ends_of(side, lane_at(0, j)))
            plane_q[p] = wq
            d = plane_d[p] + (w + wq)
            wl = edge_rows(*(harmonic0(own, edge_in[h, s, p, :1]) for s in both))
            plane_l[p] = wl
            plane_g[p] = RELAX / (d + wl)
        for c in range(COMPS):
            total = plane_num[h, p, c] + w_rad[face] * v[t][c, layer]
            total = total + plane_l[p] * edge_rows(*(edge_in[h, s, p, 1 + c : 2 + c] for s in both))
            total = total + plane_q[p] * ends_of(side, lane_at(1 + c, j))
            v[t + 1][c, slot] = (1.0 - RELAX) * v[t][c, slot] + plane_g[p] * total

    def receive(h, b):
        arrive(h, b)
        update_cols(h, b)
        update_rows(h, b)
        for p in near_planes(b):
            pl.when(rad_has[p])(functools.partial(update_plane, h, p))

    def settle(b):
        for j in range(UNROLL):
            r = b * UNROLL + j
            low, high = (row_w[s, r] for s in both)
            d = part[r] + (edge_rows(low, high) + ends_of(col_w[b], lane_at(0, j)))
            if r == 0:
                d = d + w_rad[0]
            if r == n_r - 1:
                d = d + w_rad[n_r]
            diag[r] = d
            gain[r] = RELAX / d

    def advance_face(h, b):
        t = 2 * h
        if h == 0:
            settle(b)
        for c in range(COMPS):
            for j in range(UNROLL):
                r = b * UNROLL + j
                total = num[h, c, r] + seams(t, b, j, c)
                if r in (0, n_r - 1):
                    total = total + radial(t, r, c, True)
                v[t + 1][c, r + 1] = (1.0 - RELAX) * v[t][c, r + 1] + gain[r] * total

    def first_step(h, b):
        receive(h, b)
        phase(functools.partial(advance_face, h, b))

    def whole_flux(t, b, c, j):
        r = b * UNROLL + j
        tile, near = interior(t, r, c)
        total = (f[c, r] + near) + (radial(t, r, c, None) + seams(t, b, j, c))
        return r, tile, total

    def second_step(t, b):
        for c in range(COMPS):
            for j in range(UNROLL):
                r, tile, total = whole_flux(t, b, c, j)
                v[t + 1][c, r + 1] = (1.0 - RELAX) * tile + gain[r] * total

    def residual(b):
        t = SWEEPS
        for c in range(COMPS):
            for i in range(UNROLL // 2):
                two = jnp.zeros((n_a, n_o), jnp.float32)
                for j in (2 * i, 2 * i + 1):
                    r, tile, total = whole_flux(t, b, c, j)
                    two = two + (total - diag[r] * tile)
                at = pl.ds((c * (n_r // 2) + b * (UNROLL // 2) + i) * n_a, n_a)
                for k in range(reps):
                    pairs[k, at] = two[:, k * LANES : (k + 1) * LANES]

    loaded(end)
    for b in reversed(range(blocks_r)):
        if b > 0:
            loaded(b - 1)
        phase(functools.partial(prepare, 0, b))
        if b == end:
            pl.semaphore_wait(barrier, expected)
        start(0, b)
    load_ids.wait()

    near_devices = [({"lat": lat_to[s]}, lat_has[s], lat_has[1 - s]) for s in both] + [
        ({"lon": lon_to[q]}, None, None) for q in both
    ]

    def ids_copy(i):
        return Link(functools.partial(
            pltpu.make_async_remote_copy, ids, ids_near.at[i ^ 1], ids_send.at[i], ids_recv.at[i],
            device_id=near_devices[i][0], device_id_type=MESH,
        ))

    for i, (_, send, _) in enumerate(near_devices):
        guarded(send, ids_copy(i).start)

    def wave_signal(k):
        for s in both:
            def tell():
                pl.semaphore_signal(wave.at[k, s], inc=1, device_id={"lat": lat_to[s]}, device_id_type=MESH)
            pl.when(lat_has[s])(tell)

    def wave_wait(k):
        for s in both:
            def hear():
                pl.semaphore_wait(wave.at[k, s], 1)
            pl.when(lat_has[1 - s])(hear)

    waves = n_lat - 1 if direct else 0
    if waves:
        wave_signal(0)

    lat_cell = (me_lat * n_a + row).astype(jnp.float32)
    lon_cell = (me_lon * n_o + lane_wide).astype(jnp.float32)
    phi = math.pi * ((lat_cell + 0.5) / (n_lat * n_a) - 0.5)
    lam = (2.0 * math.pi) * (lon_cell[:1] + 0.5) / (n_lon * n_o)
    cos_lat = jnp.cos(phi)
    cos_lon, sin_lon = jnp.cos(lam), jnp.sin(lam)
    rx = cos_lat * cos_lon
    ry = cos_lat * sin_lon
    rz = jnp.sin(phi)
    blocks = ids.shape[1]
    bands = n_a // FACE
    spread_rows = lax.broadcasted_iota(jnp.int32, (blocks, n_o), 0)
    spread_cols = lax.broadcasted_iota(jnp.int32, (blocks, n_o), 1)
    spread = (spread_cols // FACE == spread_rows).astype(jnp.float32)
    numbers = lax.broadcasted_iota(jnp.int32, (SLOT, n_o), 0)

    def cells_of(line, chosen):
        own = jnp.broadcast_to(line.astype(jnp.float32), (8, blocks))
        return jnp.dot(own, chosen, precision=HIGHEST)[:1]

    def hot(line):
        return hot_of(cells_of(line, spread))

    def hot_of(cells):
        return (jnp.abs(cells - numbers.astype(jnp.float32)) < 0.5).astype(jnp.float32)

    onehots = [hot(ids[band : band + 1]) for band in range(bands)]

    for k in range(1, waves):
        wave_wait(k - 1)
        wave_signal(k)

    def s1_copy(step):
        return pltpu.make_async_remote_copy(
            stage_out.at[0], lat_sums.at[me_lat], s1_send.at[0], s1_recv.at[0],
            device_id={"lat": lax.rem(me_lat + step, n_lat)}, device_id_type=MESH,
        )

    here = me_lat * n_lon + me_lon if direct else me_lon
    group = n_lat * n_lon * n_rad if direct else n_lon * n_rad
    plane = n_lon * n_rad

    def s2_copy(step):
        device = {
            "lon": lax.rem(me_lon + (step % plane) // n_rad, n_lon),
            "rad": lax.rem(me_rad + step % n_rad, n_rad),
        }
        if direct:
            device["lat"] = lax.rem(me_lat + step // plane, n_lat)
        return pltpu.make_async_remote_copy(
            stage_out.at[1], sums.at[here], s2_send.at[0], s2_recv.at[0],
            device_id=device, device_id_type=MESH,
        )

    def cross(k, x, drag):
        return [
            (x[1] * drag[2] - x[2] * drag[1]) * k,
            (x[2] * drag[0] - x[0] * drag[2]) * k,
            (x[0] * drag[1] - x[1] * drag[0]) * k,
        ]

    def torques():
        top = n_r - 1
        guess = [
            [(1.0 - RELAX) * v[2][c, r + 1] + gain[r] * num[1, c, r] for c in range(COMPS)]
            for r in (top, top - 1)
        ]
        drag = [eta[n_r] * (guess[0][c] - guess[1][c]) for c in range(COMPS)]
        twist = cross(cos_lat, (rx, ry, rz), drag) + [cos_lat]
        outer = []
        for s in both:
            k = (me_lat * n_a + (n_a if s else -1)).astype(jnp.float32)
            tilt = math.pi * ((jnp.full((1, n_o), 0.5, jnp.float32) + k) / (n_lat * n_a) - 0.5)
            cos_tilt = jnp.cos(tilt)
            moved = [row_g[s, r] * row_w[s, r] * row_out[1, s, r] for r in (top, top - 1)]
            shift = row_in[0, s, top, :1] * (moved[0] - moved[1])
            push = [shift[1 + c : 2 + c] for c in range(COMPS)]
            outer.append(cross(cos_tilt, (cos_tilt * cos_lon, cos_tilt * sin_lon, jnp.sin(tilt)), push))
        moved = col_g[end] * col_w[end] * col_out[1, end]
        shift = repeat_first(joined(col_in[0, end, 0], col_in[0, end, 1])) * (moved - turn(moved, 2 * FIELDS, 1))
        push = [ends_of(shift, lane_at(1 + c, UNROLL - 1)) for c in range(COMPS)]
        around = n_lon * n_o
        column = jnp.where(
            lane_wide[:1] == 0,
            lax.rem(me_lon * n_o + (around - 1), around), lax.rem(me_lon * n_o + n_o, around),
        ).astype(jnp.float32)
        angle = (2.0 * math.pi) * (column + 0.5) / around
        beside = cross(cos_lat, (cos_lat * jnp.cos(angle), cos_lat * jnp.sin(angle), rz), push)
        firsts = [(spread_rows == block).astype(jnp.float32) for block in (blocks - 1, 0)]
        packed = jnp.zeros((1, LANES), jnp.float32)
        for band in range(bands):
            cut = slice(band * FACE, (band + 1) * FACE)

            def stack(parts):
                return jnp.concatenate(
                    parts + [jnp.zeros((8 - len(parts), n_o), jnp.float32)], 0,
                )

            lines = [stack([jnp.sum(x[cut], axis=0, keepdims=True) for x in twist])]
            hots = [onehots[band]]
            lines.append(stack([jnp.sum(x[cut], axis=0, keepdims=True) for x in beside]))
            hots.append(hot_of(jnp.where(
                lane_wide[:1] == 0,
                cells_of(ids_near[2, band : band + 1], firsts[0]),
                cells_of(ids_near[3, band : band + 1], firsts[1]),
            )))
            for s in both:
                if band == (0, bands - 1)[s]:
                    lines.append(stack(outer[s]))
                    other = (bands - 1, 0)[s]
                    hots.append(hot(ids_near[s, other : other + 1]))
            totals = lax.dot_general(
                jnp.concatenate(lines, 1), jnp.concatenate(hots, 1), (((1,), (1,)), ((), ())),
                precision=HIGHEST, preferred_element_type=jnp.float32,
            )
            packed = packed + jnp.concatenate([totals[i : i + 1] for i in range(COMPS + 1)], 1)
        if direct:
            stage_out[1] = packed
            sums[here] = packed
            for step in range(1, group):
                s2_copy(step).start()
        else:
            stage_out[0] = packed
            lat_sums[me_lat] = packed
            for step in range(1, n_lat):
                s1_copy(step).start()

    def surface():
        if waves:
            wave_wait(waves - 1)
        for i, (_, _, take) in enumerate(near_devices):
            guarded(take, ids_copy(i).wait_recv)
        pl.when(is_top)(torques)

    def advance(b):
        phase(functools.partial(prepare, 1, b))
        if b == end:
            surface()
        start(1, b)

    def ready(b, done):
        return all(k in done for k in (b - 1, b, b + 1) if 0 <= k <= end)

    def sweep(h, order, finish, ship):
        stepped, done, shipped = set(), set(), set()
        for b in order:
            first_step(h, b)
            stepped.add(b)
            for k in order:
                if k not in done and ready(k, stepped):
                    phase(functools.partial(finish, k))
                    done.add(k)
                    for m in [end, 0] + order:
                        if ship and m not in shipped and ready(m, done):
                            ship(m)
                            shipped.add(m)

    first_order = list(reversed(range(blocks_r)))
    second_order = list(reversed(range(1, end))) + ([end, 0] if end else [0])

    def ship_off(b):
        if b == end:
            sent(0)
        advance(b)

    sweep(0, first_order, functools.partial(second_step, 1), ship_off)

    if not direct:
        @pl.when(is_top)
        def _():
            await_thin(s1_recv.at[0], n_lat - 1)
            total = lat_sums[0]
            for i in range(1, n_lat):
                total = total + lat_sums[i]
            stage_out[1] = total
            sums[here] = total
            for step in range(1, group):
                s2_copy(step).start()

    sweep(1, second_order, residual, None)

    half = n_o // 2
    thin_r = lax.broadcasted_iota(jnp.int32, (LANES, half), 0)
    thin_c = lax.broadcasted_iota(jnp.int32, (LANES, half), 1)
    count = COMPS * (n_r // 2) * n_a // 2
    merged = jnp.zeros((count, half), jnp.float32)
    for h in range(reps):
        choose = jnp.where((thin_r + h * LANES) // 2 == thin_c, 0.125, 0.0).astype(jnp.bfloat16)
        summed = pairs[h, pl.ds(0, count, stride=2)] + pairs[h, pl.ds(1, count, stride=2)]
        big = summed.astype(jnp.bfloat16)
        small = (summed - big.astype(jnp.float32)).astype(jnp.bfloat16)
        merged = merged + (
            jnp.dot(big, choose, preferred_element_type=jnp.float32)
            + jnp.dot(small, choose, preferred_element_type=jnp.float32)
        )
    mine = count // COMPS
    spot = pl.ds(pl.multiple_of(me_rad * mine, mine), mine)
    for c in range(COMPS):
        coarse[c, spot] = merged[c * mine : (c + 1) * mine]

    def g_copy(step):
        return pltpu.make_async_remote_copy(
            coarse.at[:, spot], coarse.at[:, spot], g_send.at[step - 1], g_recv.at[me_rad],
            device_id={"rad": lax.rem(me_rad + step, n_rad)}, device_id_type=MESH,
        )

    for step in range(1, n_rad):
        g_copy(step).start()

    sources = n_lat * n_lon if direct else n_lon
    pl.when(is_top)(functools.partial(await_thin, s2_recv.at[0], sources - 1))
    pl.when(jnp.logical_not(is_top))(functools.partial(await_thin, s2_recv.at[0], sources))
    terms = [sums[i] for i in range(sources)]
    while len(terms) > 1:
        terms = [terms[i] + terms[i + 1] if i + 1 < len(terms) else terms[i] for i in range(0, len(terms), 2)]
    total = terms[0]
    area = total[:, COMPS * SLOT : (COMPS + 1) * SLOT]
    valid = lax.broadcasted_iota(jnp.int32, (1, SLOT), 1) < PLATES
    root = jnp.sqrt(jnp.where(valid, area, 1.0))
    turns = jnp.concatenate(
        [total[:, i * SLOT : (i + 1) * SLOT] / root for i in range(COMPS)]
        + [jnp.zeros((8 - COMPS, SLOT), jnp.float32)], 0,
    )
    for band in range(bands):
        cut = slice(band * FACE, (band + 1) * FACE)
        cell = jnp.dot(turns, onehots[band], precision=HIGHEST, preferred_element_type=jnp.float32)
        ox, oy, oz = (cell[i : i + 1] for i in range(COMPS))
        plate[0, cut] = oy * rz[cut] - oz * ry[cut]
        plate[1, cut] = oz * rx[cut] - ox * rz[cut]
        plate[2, cut] = ox * ry[cut] - oy * rx[cut]

    sent(1)
    for i, (_, send, _) in enumerate(near_devices):
        guarded(send, ids_copy(i).wait_send)

    @pl.when(is_top)
    def _():
        if not direct:
            await_thin(s1_send.at[0], n_lat - 1, True)
        await_thin(s2_send.at[0], group - 1, True)

    for step in range(1, n_rad):
        source = lax.rem(me_rad + step, n_rad)
        region = coarse.at[:, pl.ds(pl.multiple_of(source * mine, mine), mine)]
        pltpu.make_async_remote_copy(
            region, region, g_send.at[0], g_recv.at[source],
            device_id={"rad": source}, device_id_type=MESH,
        ).wait_recv()
        g_copy(step).wait_send()


def write_out(last, coarse, plate, new_v_out, coarse_out, plate_out, sem):
    n_r = new_v_out.shape[1]
    copies = [
        pltpu.make_async_copy(last.at[:, pl.ds(1, n_r)], new_v_out, sem.at[0]),
        pltpu.make_async_copy(coarse, coarse_out, sem.at[1]),
        pltpu.make_async_copy(plate, plate_out, sem.at[2]),
    ]
    for copy in copies:
        copy.start()
    for copy in copies:
        copy.wait()


def on_device(sizes, velocity, forcing, viscosity, plate_ids):
    n_lat, n_lon, n_rad = sizes
    _, n_r, n_a, n_o = velocity.shape
    chunks = n_r // UNROLL
    f32 = jnp.float32
    dma = pltpu.SemaphoreType.DMA
    direct = n_lat * n_lon * n_rad <= DIRECT
    group = n_lat * n_lon * n_rad if direct else n_lon * n_rad
    sources = n_lat * n_lon if direct else n_lon
    in_any = pl.BlockSpec(memory_space=pl.ANY)
    in_vmem = pl.BlockSpec(memory_space=pltpu.VMEM)
    coarse_rows = n_rad * (n_r // 2) * (n_a // 2)
    whole = (n_r, n_a, n_o)
    thin = (n_a, LANES)

    def vmem(*shape):
        return pltpu.VMEM(shape, f32)

    held = pl.pallas_call(
        functools.partial(kernel, sizes),
        out_shape=(
            pltpu.VMEM((COMPS, n_r + 2, n_a, n_o), f32),
            pltpu.VMEM((COMPS, coarse_rows, n_o // 2), f32),
            pltpu.VMEM((COMPS, n_a, n_o), f32),
        ),
        in_specs=[pl.BlockSpec(memory_space=pltpu.HBM)] * 4,
        out_specs=(in_vmem,) * 3,
        scratch_shapes=[
            vmem(SWEEPS, COMPS, n_r + 2, n_a, n_o),
            pltpu.VMEM(plate_ids.shape, jnp.int32),
            pltpu.VMEM((4,) + plate_ids.shape, jnp.int32),
            vmem(COMPS, *whole),
            vmem(n_r + 2, n_a, n_o),
            vmem(2, *whole),
            vmem(2, *whole),
            vmem(n_r + 1, n_a, n_o),
            vmem(*whole),
            vmem(*whole),
            vmem(*whole),
            vmem(2, COMPS, *whole),
            vmem(2, 2, *whole),
            vmem(2, 2, *whole),
            vmem(4, 2, *whole),
            vmem(2, n_r, 1, n_o),
            vmem(2, n_r, 1, n_o),
            vmem(2, n_r, 1, n_o),
            vmem(2, 2, 1, n_o),
            vmem(2, chunks, *thin),
            vmem(2, chunks, 2, *thin),
            vmem(4, chunks, *thin),
            vmem(chunks, *thin),
            vmem(chunks, *thin),
            vmem(chunks, 2, *thin),
            vmem(2, *thin),
            vmem(2, 2, COMPS, n_a, n_o),
            vmem(2, n_a, n_o),
            vmem(2, n_a, n_o),
            vmem(2, n_a, n_o),
            vmem(2, n_a, n_o),
            vmem(2, chunks, 2, 1, LANES),
            vmem(2, chunks, 2, 2, 1, LANES),
            vmem(2, chunks, LANES, 8),
            vmem(2, 2, 2, n_a, n_o),
            vmem(2, 2, 2, *thin),
            vmem(n_o // LANES, COMPS * (n_r // 2) * n_a, LANES),
            vmem(sources, 1, LANES),
            vmem(n_lat, 1, LANES),
            vmem(2, 1, LANES),
            vmem(max(7 * UNROLL * n_a, chunks * (UNROLL * FIELDS + 8)), 1, n_o),
            vmem(max(group, sources, n_lat), 1, LANES),
            dma((chunks + 1,)),
            dma((1,)),
            dma((2,)),
            dma((2,)),
            dma((2, 2)),
            dma((2, chunks)),
            dma((2, chunks, 2)),
            dma((2, 2)),
            dma((2, 2, 2)),
            dma((4,)),
            dma((4,)),
            pltpu.SemaphoreType.REGULAR((n_lat - 1 if direct else 1, 2)),
            dma((1,)),
            dma((1,)),
            dma((1,)),
            dma((1,)),
            dma((n_rad,)),
            dma((n_rad,)),
        ],
        compiler_params=pltpu.CompilerParams(
            collective_id=0, has_side_effects=True, vmem_limit_bytes=32 * 2**20
        ),
    )(*(
        pltpu.with_memory_space_constraint(x, pltpu.HBM)
        for x in (velocity, forcing, viscosity, plate_ids)
    ))
    new_v, coarse, plate = pl.pallas_call(
        write_out,
        out_shape=(
            jax.ShapeDtypeStruct(velocity.shape, f32),
            jax.ShapeDtypeStruct((COMPS, coarse_rows, n_o // 2), f32),
            jax.ShapeDtypeStruct((COMPS, n_a, n_o), f32),
        ),
        in_specs=[in_vmem] * 3,
        out_specs=(in_any,) * 3,
        scratch_shapes=[dma((3,))],
        compiler_params=pltpu.CompilerParams(vmem_limit_bytes=4 * 2**20),
    )(*(pltpu.with_memory_space_constraint(x, pltpu.VMEM) for x in held))
    coarse = coarse.reshape(COMPS, n_rad * (n_r // 2), n_a // 2, n_o // 2)
    return new_v, coarse, plate


def solution(mesh):
    sizes = tuple(mesh.shape[a] for a in ("lat", "lon", "rad"))
    field = P(None, "rad", "lat", "lon")
    return jax.shard_map(
        functools.partial(on_device, sizes),
        mesh=mesh,
        in_specs=(field, field, P("rad", "lat", "lon"), P("lat", "lon")),
        out_specs=(field, P(None, None, "lat", "lon"), P(None, "lat", "lon")),
        check_vma=False,
    )
```

time: 23.6 us -> 21.3 us (0.903)
  Pallas kernels: 22.8 us -> 20.5 us
    pallas_call x1, Pallas kernels: 22 us -> 19.7 us  [on_device(): pl.pallas_call(functools.partial(kernel, sizes), out_shape=(pltpu.VMEM((C...]
where the time goes in v1:
time: 21.3 us; the launch traced here: 21.1 us
  Pallas kernels  20.5 us (96%)
  between operations  0.64 us (3%)
    pallas_call x1, Pallas kernels, on_device(): pl.pallas_call(functools.partial(kernel, sizes), out_shape=(pltpu.VMEM((C...  19.7 us
    pallas_call x1, Pallas kernels, on_device(): pl.pallas_call(write_out, out_shape=(jax.ShapeDtypeStruct(velocity.shape,...  0.8 us

profile of v1, /device:TPU:0, one launch (start us, length us, event | category | flops | bytes accessed | tf_op | source)
XLA Modules:
  0.0 21.1 jit_solution(1840304618632205751)
XLA Ops:
  0.6 19.7 %shard_map.67 = (f32[3,18,8,256]{3,2,1,0:T(8,128)S(1)}, f32[3,64,128]{2,1,0:T(8,128)S(1)}, f32[3,8,256]{2,1,0:T(8,128)S(1)}) custom-call(f32[3,16,8,256]{3,2,1,0:T(8,128)} %vel.1, f32[3,16,8,256]{3,2,1,0:T(8,128)} %forc.1, f32[16,8,256]{2,1,0:T(8,128)} %visc.1, s32[1,32]{1,0:T(1,128)} %ids_in.1), custom_call_target="tpu_custom_call" | custom-call | tf_op jit(solution)/shard_map/pallas_call | solution.py:863
  20.3 0.8 %shard_map.68 = (f32[3,16,8,256]{3,2,1,0:T(8,128)}, f32[3,64,128]{2,1,0:T(8,128)}, f32[3,8,256]{2,1,0:T(8,128)}) custom-call(f32[3,18,8,256]{3,2,1,0:T(8,128)S(1)} %get-tuple-element.9.last, f32[3,64,128]{2,1,0:T(8,128)S(1)} %get-tuple-element.10.coarse, f32[3,8,256]{2,1,0:T(8,128)S(1)} %get-tuple-element.11.plate), custom_call_target="tpu_custom_call" | custom-call | tf_op jit(solution)/shard_map/pallas_call | solution.py:941

commit v2 on v1

--- a/solution.py
+++ b/solution.py
@@ -17,7 +17,7 @@
 SLOT = 32
 MESH = pl.DeviceIdType.MESH
 HIGHEST = lax.Precision.HIGHEST
-UNROLL = 4
+UNROLL = 8
 DIRECT = 64
 FIELDS = 2 * (COMPS + 1)
 
@@ -49,11 +49,11 @@
     last, coarse, plate,
     early, ids, ids_near, f, eta, w_lat, w_lon, w_rad, gain, diag, part, num,
     row_out, row_in, row_sum, row_w, row_g, row_q, row_p,
-    col_out, col_in, col_sum, col_w, col_g, col_d, col_p,
+    col_first, col_out, col_in, col_far, col_sum, col_w, col_g, col_d, col_p,
     plane_num, plane_d, plane_g, plane_l, plane_q,
-    corner_out, corner_in, corner_t, edge_in, side_in,
+    corner_out, corner_in, corner_t, edge_out, edge_in, side_in,
     pairs, sums, lat_sums, stage_out, tally, tally_thin,
-    load_sem, lon_send, lat_send, rad_send, edge_send, lon_recv, lat_recv, rad_recv, edge_recv,
+    load_sem, lon_send, lat_send, rad_send, num_send, edge_send, lon_recv, lat_recv, rad_recv, num_recv, edge_recv, far_send, far_recv,
     ids_send, ids_recv, wave, s1_send, s1_recv, s2_send, s2_recv, g_send, g_recv,
 ):
     n_lat, n_lon, n_rad = sizes
@@ -188,7 +188,7 @@
                     edge_in[h, s, p] = jnp.zeros((n_a, n_o), jnp.float32)
             ids_near[s] = jnp.zeros(ids.shape, jnp.int32)
 
-    def messages(h, b):
+    def messages(h, b, early_part):
         t = 2 * h
         table = []
 
@@ -201,36 +201,43 @@
         for p, layer, slot in ((0, 1, n_r + 1), (1, n_r, 0)):
             if p not in near_planes(b):
                 continue
-            sems = (rad_send.at[p], rad_recv.at[h, 1 - p])
             device = {"rad": rad_to[p]}
-            add(v[t].at[:, layer], v[t].at[:, slot], *sems, device, rad_has[p])
-            add(num.at[h, :, layer - 1], plane_num.at[h, 1 - p], *sems, device, rad_has[p])
-            if h == 0:
-                add(eta.at[layer], eta.at[slot], *sems, device, rad_has[p])
-                add(part.at[layer - 1], plane_d.at[1 - p], *sems, device, rad_has[p])
-            for q in both:
-                add(
-                    col_out.at[h, b], side_in.at[h, 1 - p, 1 - q], *sems,
-                    {"lon": lon_to[q], "rad": rad_to[p]}, rad_has[p],
-                )
+            if early_part:
+                sems = (rad_send.at[p], rad_recv.at[h, 1 - p])
+                add(v[t].at[:, layer], v[t].at[:, slot], *sems, device, rad_has[p])
+                if h == 0:
+                    add(eta.at[layer], eta.at[slot], *sems, device, rad_has[p])
+            sems = (num_send.at[p], num_recv.at[h, 1 - p])
+            if early_part:
+                for q in both:
+                    add(
+                        col_first.at[h, b], side_in.at[h, 1 - p, 1 - q], *sems,
+                        {"lon": lon_to[q], "rad": rad_to[p]}, rad_has[p],
+                    )
+                for s in both:
+                    add(
+                        edge_out.at[h, s, p], edge_in.at[h, 1 - s, 1 - p],
+                        edge_send.at[s, p], edge_recv.at[h, 1 - s, 1 - p],
+                        {"lat": lat_to[s], "rad": rad_to[p]}, all_of(rad_has[p], lat_has[s]),
+                    )
+            else:
+                add(num.at[h, :, layer - 1], plane_num.at[h, 1 - p], *sems, device, rad_has[p])
+                if h == 0:
+                    add(part.at[layer - 1], plane_d.at[1 - p], *sems, device, rad_has[p])
+        if early_part:
             for s in both:
-                add(
-                    row_out.at[h, s, layer - 1], edge_in.at[h, 1 - s, 1 - p],
-                    edge_send.at[s, p], edge_recv.at[h, 1 - s, 1 - p],
-                    {"lat": lat_to[s], "rad": rad_to[p]}, all_of(rad_has[p], lat_has[s]),
-                )
+                for q in both:
+                    add(
+                        corner_out.at[h, b, s], corner_in.at[h, b, 1 - s, 1 - q],
+                        far_send.at[s], far_recv.at[h, 1 - s],
+                        {"lat": lat_to[s], "lon": lon_to[q]}, lat_has[s],
+                    )
+            return table
         for q in both:
             add(
                 col_out.at[h, b], col_in.at[h, b, 1 - q], lon_send.at[0], lon_recv.at[h, b],
                 {"lon": lon_to[q]}, None,
             )
-        for s in both:
-            for q in both:
-                add(
-                    corner_out.at[h, b, s], corner_in.at[h, b, 1 - s, 1 - q],
-                    lat_send.at[s], lat_recv.at[h, b, 1 - s],
-                    {"lat": lat_to[s], "lon": lon_to[q]}, lat_has[s],
-                )
         layers = pl.ds(b * UNROLL, UNROLL)
         for s in both:
             add(
@@ -240,33 +247,45 @@
         return table
 
     corner_rows = 2 * LANES // n_o
-    lat_rows = UNROLL * FIELDS + corner_rows
+    lat_rows = UNROLL * FIELDS
 
     def rad_rows(h):
-        return (2 * COMPS + (2 if h == 0 else 0)) * n_a + 2 * tile_rows
-
-    def start(h, b):
-        for copy, cond in messages(h, b):
+        return (COMPS + (1 if h == 0 else 0)) * n_a
+
+    def num_rows(h):
+        return rad_rows(h) + 2 * tile_rows
+
+    def start(h, b, early_part=False):
+        for copy, cond in messages(h, b, early_part):
             guarded(cond, copy.start)
 
     def near_planes(b):
         return [p for p, at in ((0, 0), (1, end)) if b == at]
 
     def arrive(h, b):
-        for p in near_planes(b):
+        await_rows(lon_recv.at[h, b], 2 * tile_rows)
+        for s in both:
+            guarded(lat_has[s], functools.partial(await_rows, lat_recv.at[h, b, s], lat_rows))
+
+    def arrive_far(h):
+        for p in both:
             guarded(rad_has[p], functools.partial(await_rows, rad_recv.at[h, p], rad_rows(h)))
-            for s in both:
+            guarded(rad_has[p], functools.partial(await_rows, num_recv.at[h, p], num_rows(h)))
+        for s in both:
+            for p in both:
                 guarded(
                     all_of(rad_has[p], lat_has[s]),
                     functools.partial(await_rows, edge_recv.at[h, s, p], FIELDS),
                 )
-        await_rows(lon_recv.at[h, b], 2 * tile_rows)
-        for s in both:
-            guarded(lat_has[s], functools.partial(await_rows, lat_recv.at[h, b, s], lat_rows))
+            guarded(
+                lat_has[s],
+                functools.partial(await_rows, far_recv.at[h, s], blocks_r * corner_rows),
+            )
 
     def sent(h):
         for p in both:
             guarded(rad_has[p], functools.partial(await_rows, rad_send.at[p], rad_rows(h), True))
+            guarded(rad_has[p], functools.partial(await_rows, num_send.at[p], num_rows(h), True))
             for s in both:
                 guarded(
                     all_of(rad_has[p], lat_has[s]),
@@ -275,6 +294,7 @@
         await_rows(lon_send.at[0], blocks_r * 2 * tile_rows, True)
         for s in both:
             guarded(lat_has[s], functools.partial(await_rows, lat_send.at[s], blocks_r * lat_rows, True))
+            guarded(lat_has[s], functools.partial(await_rows, far_send.at[s], blocks_r * corner_rows, True))
 
     def turn(x, shift, axis):
         shift = shift % x.shape[axis]
@@ -316,16 +336,38 @@
         return edge_rows(low, high) + ends_of(col_sum[t, b], lane_at(1 + c, j))
 
     def pack(h, r, k, tile, packed):
-        row_out[h, 0, r, k : k + 1, :] = tile[:1]
-        row_out[h, 1, r, k : k + 1, :] = tile[n_a - 1 :]
+        for i in range(reps):
+            piece = slice(i * LANES, (i + 1) * LANES)
+            row_out[h, 0, r, k : k + 1, piece] = tile[:1, piece]
+            row_out[h, 1, r, k : k + 1, piece] = tile[n_a - 1 :, piece]
         at = lane_at(k, r % UNROLL)
         two = jnp.where(lane < LANES // 2, tile[:, :LANES], tile[:, n_o - LANES :])
         hit = jnp.logical_and(field_of == k, layer_of == r % UNROLL)
         return jnp.where(hit, turn(two, at, 1), packed)
 
+    def pack_first(h, b):
+        t = 2 * h
+        packed = jnp.zeros((n_a, LANES), jnp.float32)
+        for j in range(UNROLL):
+            r = b * UNROLL + j
+            tiles = [(1 + c, v[t][c, r + 1]) for c in range(COMPS)]
+            if h == 0:
+                tiles.append((0, eta[r + 1]))
+            for k, tile in tiles:
+                packed = pack(h, r, k, tile, packed)
+                for p, layer in ((0, 0), (1, n_r - 1)):
+                    if r == layer:
+                        for s in both:
+                            for i in range(reps):
+                                piece = slice(i * LANES, (i + 1) * LANES)
+                                edge_out[h, s, p, k : k + 1, piece] = tile[row_edge[s] : row_edge[s] + 1, piece]
+        col_first[h, b] = packed
+        for s in both:
+            corner_out[h, b, s] = packed[row_edge[s] : row_edge[s] + 1]
+
     def prepare(h, b):
         t = 2 * h
-        packed = jnp.zeros((n_a, LANES), jnp.float32)
+        packed = col_first[h, b]
         for j in range(UNROLL):
             r = b * UNROLL + j
             if h == 0:
@@ -346,7 +388,6 @@
                 if r < n_r - 1:
                     d = d + harmonic(own, eta[r + 2])
                 part[r] = d
-                packed = pack(h, r, 0, own, packed)
                 packed = pack(h, r, FIELDS - 1, d, packed)
         for j in range(UNROLL):
             r = b * UNROLL + j
@@ -362,11 +403,8 @@
                 else:
                     total = f[c, r] + (near + radial(t, r, c, False))
                 num[h, c, r] = total
-                packed = pack(h, r, 1 + c, tile, packed)
                 packed = pack(h, r, 1 + COMPS + c, total, packed)
         col_out[h, b] = packed
-        for s in both:
-            corner_out[h, b, s] = packed[row_edge[s] : row_edge[s] + 1]
 
     def repeat_from(x, field, shifts):
         fields = field_of if x.shape[0] == n_a else field_of[:1]
@@ -383,59 +421,75 @@
         at = even if from_west.shape[0] == n_a else even[:1]
         return jnp.where(at, turn(from_west, 1, 1), turn(from_east, -1, 1))
 
-    def update_rows(h, b):
+    def near_side(h, b):
         t = 2 * h
-        stacked = jnp.zeros((8, LANES), jnp.float32)
-        spot = lax.broadcasted_iota(jnp.int32, (8, LANES), 0)
-        for s in both:
-            stacked = jnp.where(spot == 2 * s, turn(corner_in[h, b, s, 0], 1, 1), stacked)
-            stacked = jnp.where(spot == 2 * s + 1, corner_in[h, b, s, 1], stacked)
-        corner_t[h, b] = stacked.T
+        far = joined(col_in[h, b, 0], col_in[h, b, 1])
+        col_far[h, b] = far
+        if h == 0:
+            w = harmonic0(repeat_first(far), repeat_first(col_out[h, b]))
+            col_w[b] = w
+        else:
+            w = col_w[b]
+        col_sum[t, b] = w * far
+        for s in both:
+            for r in range(b * UNROLL, (b + 1) * UNROLL):
+                if h == 0:
+                    w = harmonic(
+                        jnp.broadcast_to(row_in[h, s, r, :1], (n_a, n_o)),
+                        jnp.broadcast_to(row_out[h, s, r, :1], (n_a, n_o)),
+                    )
+                    row_w[s, r] = w
+                else:
+                    w = row_w[s, r]
+                row_sum[t, s, r] = w * row_in[h, s, r]
+
+    def far_rows(h, b):
+        t = 2 * h
         for s in both:
             for j in range(UNROLL):
                 r = b * UNROLL + j
-                own, far = row_out[h, s, r], row_in[h, s, r]
+                far = row_in[h, s, r]
                 column = corner_t[h, b, pl.ds(lane_at(0, j), FIELDS, stride=2), :]
-                west = jnp.where(lane == 0, column[:, 2 * s : 2 * s + 1], 0.0)
-                east = jnp.where(lane == LANES - 1, column[:, 2 * s + 1 : 2 * s + 2], 0.0)
-                if reps == 1:
-                    corner = west + east
-                else:
-                    gap = [jnp.zeros((n_a, LANES), jnp.float32)] * (reps - 2)
-                    corner = jnp.concatenate([west] + gap + [east], 1)
+                corner = ends_of(column, 2 * s + 1)
                 near = [p for p, layer in ((0, 0), (1, n_r - 1)) if r == layer]
+                w = row_w[s, r]
                 if h == 0:
-                    far_eta = far[:1]
-                    w = harmonic(far_eta, own[:1])
+                    far_eta = jnp.broadcast_to(row_in[h, s, r, :1], (n_a, n_o))
                     wq = harmonic0(far_eta, corner[:1])
-                    d = far[FIELDS - 1 :] + (w + wq)
+                    d = row_in[h, s, r, FIELDS - 1 :] + (w + wq)
                     for p in near:
                         wp = harmonic0(far_eta, edge_in[h, s, p, :1])
                         row_p[s, p] = wp
                         d = d + wp
-                    row_w[s, r] = w
                     row_q[s, r] = wq
-                    row_g[s, r] = RELAX / d
-                w = row_w[s, r]
-                total = turn(far, -COMPS, 0) + w * own + row_q[s, r] * corner
+                    gain_far = RELAX / d
+                    row_g[s, r] = gain_far
+                else:
+                    wq, gain_far = row_q[s, r], row_g[s, r]
+                total = turn(far, -COMPS, 0) + w * row_out[h, s, r] + wq * corner
                 for p in near:
                     total = total + row_p[s, p] * edge_in[h, s, p]
-                row_sum[t, s, r] = w * far
-                row_sum[t + 1, s, r] = w * ((1.0 - RELAX) * far + row_g[s, r] * total)
+                row_sum[t + 1, s, r] = w * ((1.0 - RELAX) * far + gain_far * total)
 
     def side_of(h, p):
         return joined(side_in[h, p, 0], side_in[h, p, 1])
 
-    def update_cols(h, b):
+    def far_cols(h, b):
         t = 2 * h
-        far = joined(col_in[h, b, 0], col_in[h, b, 1])
+        far = col_far[h, b]
         own = col_out[h, b]
+        stacked = jnp.zeros((8, LANES), jnp.float32)
+        spot = lax.broadcasted_iota(jnp.int32, (8, LANES), 0)
+        for s in both:
+            stacked = jnp.where(spot == 2 * s + 1, turn(corner_in[h, b, s, 0], 1, 1), stacked)
+            stacked = jnp.where(spot == 2 * s, corner_in[h, b, s, 1], stacked)
+        corner_t[h, b, :, :8] = stacked.T
         corners = [joined(corner_in[h, b, s, 0], corner_in[h, b, s, 1]) for s in both]
         move = 2 * FIELDS * (UNROLL - 1)
         sides = {p: turn(side_of(h, p), -move if p == 0 else move, 1) for p in near_planes(b)}
+        w = col_w[b]
         if h == 0:
             far_eta = repeat_first(far)
-            w = harmonic0(far_eta, repeat_first(own))
             d = repeat_last(far) + w
             for s in both:
                 wd = jnp.where(
@@ -449,16 +503,17 @@
                 )
                 col_p[p] = wp
                 d = d + wp
-            col_w[b] = w
             col_g[b] = RELAX / jnp.where(d > 0.0, d, 1.0)
-        w = col_w[b]
         total = turn(far, -2 * COMPS, 1) + w * own
         for s in both:
             total = total + col_d[b, s] * corners[s]
         for p in near_planes(b):
             total = total + col_p[p] * sides[p]
-        col_sum[t, b] = w * far
         col_sum[t + 1, b] = w * ((1.0 - RELAX) * far + col_g[b] * total)
+
+    def link_plane(p):
+        slot, layer, face = ((0, 1, 0), (n_r + 1, n_r, n_r))[p]
+        w_rad[face] = harmonic(eta[slot], eta[layer])
 
     def update_plane(h, p):
         t = 2 * h
@@ -466,8 +521,7 @@
         side = side_of(h, p)
         if h == 0:
             own = eta[slot]
-            w = harmonic(own, eta[layer])
-            w_rad[face] = w
+            w = w_rad[face]
             wq = harmonic0(own, ends_of(side, lane_at(0, j)))
             plane_q[p] = wq
             d = plane_d[p] + (w + wq)
@@ -480,17 +534,10 @@
             total = total + plane_q[p] * ends_of(side, lane_at(1 + c, j))
             v[t + 1][c, slot] = (1.0 - RELAX) * v[t][c, slot] + plane_g[p] * total
 
-    def receive(h, b):
-        arrive(h, b)
-        update_cols(h, b)
-        update_rows(h, b)
-        for p in near_planes(b):
-            pl.when(rad_has[p])(functools.partial(update_plane, h, p))
-
     def settle(b):
         for j in range(UNROLL):
             r = b * UNROLL + j
-            low, high = (row_w[s, r] for s in both)
+            low, high = (row_w[s, r, :1] for s in both)
             d = part[r] + (edge_rows(low, high) + ends_of(col_w[b], lane_at(0, j)))
             if r == 0:
                 d = d + w_rad[0]
@@ -511,10 +558,6 @@
                     total = total + radial(t, r, c, True)
                 v[t + 1][c, r + 1] = (1.0 - RELAX) * v[t][c, r + 1] + gain[r] * total
 
-    def first_step(h, b):
-        receive(h, b)
-        phase(functools.partial(advance_face, h, b))
-
     def whole_flux(t, b, c, j):
         r = b * UNROLL + j
         tile, near = interior(t, r, c)
@@ -539,13 +582,14 @@
                 for k in range(reps):
                     pairs[k, at] = two[:, k * LANES : (k + 1) * LANES]
 
-    loaded(end)
     for b in reversed(range(blocks_r)):
-        if b > 0:
-            loaded(b - 1)
+        loaded(b)
+        phase(functools.partial(pack_first, 0, b))
+    pl.semaphore_wait(barrier, expected)
+    for b in reversed(range(blocks_r)):
+        start(0, b, True)
+    for b in reversed(range(blocks_r)):
         phase(functools.partial(prepare, 0, b))
-        if b == end:
-            pl.semaphore_wait(barrier, expected)
         start(0, b)
     load_ids.wait()
 
@@ -652,12 +696,12 @@
             k = (me_lat * n_a + (n_a if s else -1)).astype(jnp.float32)
             tilt = math.pi * ((jnp.full((1, n_o), 0.5, jnp.float32) + k) / (n_lat * n_a) - 0.5)
             cos_tilt = jnp.cos(tilt)
-            moved = [row_g[s, r] * row_w[s, r] * row_out[1, s, r] for r in (top, top - 1)]
+            moved = [(row_g[s, r] * row_w[s, r]) * row_out[1, s, r] for r in (top, top - 1)]
             shift = row_in[0, s, top, :1] * (moved[0] - moved[1])
             push = [shift[1 + c : 2 + c] for c in range(COMPS)]
             outer.append(cross(cos_tilt, (cos_tilt * cos_lon, cos_tilt * sin_lon, jnp.sin(tilt)), push))
         moved = col_g[end] * col_w[end] * col_out[1, end]
-        shift = repeat_first(joined(col_in[0, end, 0], col_in[0, end, 1])) * (moved - turn(moved, 2 * FIELDS, 1))
+        shift = repeat_first(col_far[0, end]) * (moved - turn(moved, 2 * FIELDS, 1))
         push = [ends_of(shift, lane_at(1 + c, UNROLL - 1)) for c in range(COMPS)]
         around = n_lon * n_o
         column = jnp.where(
@@ -723,24 +767,44 @@
 
     def sweep(h, order, finish, ship):
         stepped, done, shipped = set(), set(), set()
-        for b in order:
-            first_step(h, b)
+
+        def near_part(b):
+            near_side(h, b)
+            far_cols(h, b)
+
+        def main_part(b):
+            advance_face(h, b)
+            far_rows(h, b)
+
+        for at, b in enumerate(order):
+            arrive(h, b)
+            if at == 0:
+                arrive_far(h)
+                for p in both:
+                    if h == 0:
+                        pl.when(rad_has[p])(functools.partial(link_plane, p))
+                    pl.when(rad_has[p])(functools.partial(update_plane, h, p))
+            phase(functools.partial(near_part, b))
+            phase(functools.partial(main_part, b))
             stepped.add(b)
             for k in order:
                 if k not in done and ready(k, stepped):
                     phase(functools.partial(finish, k))
                     done.add(k)
+                    if ship:
+                        if k == end:
+                            sent(0)
+                        phase(functools.partial(pack_first, 1, k))
+                        start(1, k, True)
                     for m in [end, 0] + order:
                         if ship and m not in shipped and ready(m, done):
                             ship(m)
                             shipped.add(m)
 
     first_order = list(reversed(range(blocks_r)))
-    second_order = list(reversed(range(1, end))) + ([end, 0] if end else [0])
+    second_order = [end] + list(reversed(range(2, end))) + [k for k in (0, 1) if k < end]
 
     def ship_off(b):
-        if b == end:
-            sent(0)
         advance(b)
 
     sweep(0, first_order, functools.partial(second_step, 1), ship_off)
@@ -885,12 +949,14 @@
             vmem(2, 2, *whole),
             vmem(2, 2, *whole),
             vmem(4, 2, *whole),
-            vmem(2, n_r, 1, n_o),
-            vmem(2, n_r, 1, n_o),
-            vmem(2, n_r, 1, n_o),
-            vmem(2, 2, 1, n_o),
+            vmem(2, *whole),
+            vmem(2, *whole),
+            vmem(2, *whole),
+            vmem(2, 2, n_a, n_o),
+            vmem(2, chunks, *thin),
             vmem(2, chunks, *thin),
             vmem(2, chunks, 2, *thin),
+            vmem(2, chunks, *thin),
             vmem(4, chunks, *thin),
             vmem(chunks, *thin),
             vmem(chunks, *thin),
@@ -903,7 +969,8 @@
             vmem(2, n_a, n_o),
             vmem(2, chunks, 2, 1, LANES),
             vmem(2, chunks, 2, 2, 1, LANES),
-            vmem(2, chunks, LANES, 8),
+            vmem(2, chunks, LANES, LANES),
+            vmem(2, 2, 2, n_a, n_o),
             vmem(2, 2, 2, n_a, n_o),
             vmem(2, 2, 2, *thin),
             vmem(n_o // LANES, COMPS * (n_r // 2) * n_a, LANES),
@@ -916,11 +983,15 @@
             dma((1,)),
             dma((2,)),
             dma((2,)),
+            dma((2,)),
             dma((2, 2)),
             dma((2, chunks)),
             dma((2, chunks, 2)),
             dma((2, 2)),
+            dma((2, 2)),
             dma((2, 2, 2)),
+            dma((2,)),
+            dma((2, 2)),
             dma((4,)),
             dma((4,)),
             pltpu.SemaphoreType.REGULAR((n_lat - 1 if direct else 1, 2)),

time: 21.3 us -> 20.5 us (0.962)
  Pallas kernels: 20.5 us -> 19.7 us
    pallas_call x1, Pallas kernels: 19.7 us -> 18.9 us  [on_device(): pl.pallas_call(functools.partial(kernel, sizes), out_shape=(pltpu.VMEM((C...]
where the time goes in v2:
time: 20.5 us; the launch traced here: 20.3 us
  Pallas kernels  19.7 us (96%)
  between operations  0.64 us (3%)
    pallas_call x1, Pallas kernels, on_device(): pl.pallas_call(functools.partial(kernel, sizes), out_shape=(pltpu.VMEM((C...  18.9 us
    pallas_call x1, Pallas kernels, on_device(): pl.pallas_call(write_out, out_shape=(jax.ShapeDtypeStruct(velocity.shape,...  0.8 us

profile of v2, /device:TPU:0, one launch (start us, length us, event | category | flops | bytes accessed | tf_op | source)
XLA Modules:
  0.0 20.3 jit_solution(9621428702982800232)
XLA Ops:
  0.6 18.9 %shard_map.67 = (f32[3,18,8,256]{3,2,1,0:T(8,128)S(1)}, f32[3,64,128]{2,1,0:T(8,128)S(1)}, f32[3,8,256]{2,1,0:T(8,128)S(1)}) custom-call(f32[3,16,8,256]{3,2,1,0:T(8,128)} %vel.1, f32[3,16,8,256]{3,2,1,0:T(8,128)} %forc.1, f32[16,8,256]{2,1,0:T(8,128)} %visc.1, s32[1,32]{1,0:T(1,128)} %ids_in.1), custom_call_target="tpu_custom_call" | custom-call | tf_op jit(solution)/shard_map/pallas_call | solution.py:927
  19.5 0.8 %shard_map.68 = (f32[3,16,8,256]{3,2,1,0:T(8,128)}, f32[3,64,128]{2,1,0:T(8,128)}, f32[3,8,256]{2,1,0:T(8,128)}) custom-call(f32[3,18,8,256]{3,2,1,0:T(8,128)S(1)} %get-tuple-element.9.last, f32[3,64,128]{2,1,0:T(8,128)S(1)} %get-tuple-element.10.coarse, f32[3,8,256]{2,1,0:T(8,128)S(1)} %get-tuple-element.11.plate), custom_call_target="tpu_custom_call" | custom-call | tf_op jit(solution)/shard_map/pallas_call | solution.py:1012

commit v3 on v2

--- a/solution.py
+++ b/solution.py
@@ -20,6 +20,7 @@
 UNROLL = 8
 DIRECT = 64
 FIELDS = 2 * (COMPS + 1)
+PACK = COMPS + 1
 
 
 def harmonic(own, other):
@@ -48,12 +49,12 @@
     sizes, vel, forc, visc, ids_in,
     last, coarse, plate,
     early, ids, ids_near, f, eta, w_lat, w_lon, w_rad, gain, diag, part, num,
-    row_out, row_in, row_sum, row_w, row_g, row_q, row_p,
+    row_out, row_in, more_out, more_in, row_sum, row_w, row_g, row_q, row_p,
     col_first, col_out, col_in, col_far, col_sum, col_w, col_g, col_d, col_p,
     plane_num, plane_d, plane_g, plane_l, plane_q,
     corner_out, corner_in, corner_t, edge_out, edge_in, side_in,
     pairs, sums, lat_sums, stage_out, tally, tally_thin,
-    load_sem, lon_send, lat_send, rad_send, num_send, edge_send, lon_recv, lat_recv, rad_recv, num_recv, edge_recv, far_send, far_recv,
+    load_sem, lon_send, lat_send, rad_send, num_send, edge_send, lon_recv, lat_recv, late_lon_send, late_lat_send, late_lon_recv, late_lat_recv, rad_recv, num_recv, edge_recv, far_send, far_recv,
     ids_send, ids_recv, wave, s1_send, s1_recv, s2_send, s2_recv, g_send, g_recv,
 ):
     n_lat, n_lon, n_rad = sizes
@@ -108,19 +109,21 @@
             greet({"lat": lax.rem(me_lat + step, n_lat)})
         expected = expected + (n_lat - 1)
 
-    def load_chunk(b):
+    def load_chunk(b, rest):
         here_r = pl.ds(b * UNROLL, UNROLL)
         inner = pl.ds(1 + b * UNROLL, UNROLL)
+        if rest:
+            return [pltpu.make_async_copy(forc.at[:, here_r], f.at[:, here_r], load_sem.at[blocks_r + b])]
         return [
             pltpu.make_async_copy(visc.at[here_r], eta.at[inner], load_sem.at[b]),
             pltpu.make_async_copy(vel.at[:, here_r], v[0].at[:, inner], load_sem.at[b]),
-            pltpu.make_async_copy(forc.at[:, here_r], f.at[:, here_r], load_sem.at[b]),
         ]
 
-    for b in reversed(range(blocks_r)):
-        for load in load_chunk(b):
-            load.start()
-    load_ids = pltpu.make_async_copy(ids_in, ids, load_sem.at[blocks_r])
+    for rest in (False, True):
+        for b in reversed(range(blocks_r)):
+            for load in load_chunk(b, rest):
+                load.start()
+    load_ids = pltpu.make_async_copy(ids_in, ids, load_sem.at[2 * blocks_r])
     load_ids.start()
 
     def rows_of(ref):
@@ -140,9 +143,10 @@
         )
         copy.wait_send() if sending else copy.wait_recv()
 
-    def loaded(b):
-        some = tally.at[pl.ds(0, (2 * COMPS + 1) * UNROLL * n_a)]
-        pltpu.make_async_copy(some, some, load_sem.at[b]).wait()
+    def loaded(b, rest=False):
+        fields = COMPS if rest else COMPS + 1
+        some = tally.at[pl.ds(0, fields * UNROLL * n_a)]
+        pltpu.make_async_copy(some, some, load_sem.at[blocks_r + b if rest else b]).wait()
 
     lane_wide = lax.broadcasted_iota(jnp.int32, (n_a, n_o), 1)
     lane = lax.broadcasted_iota(jnp.int32, (n_a, LANES), 1)
@@ -172,20 +176,21 @@
                     v[t][c, slot] = zero_plane
             for h in both:
                 for s in both:
-                    edge_in[h, s, p] = zero_plane
+                    edge_in[h, s, p] = jnp.zeros((PACK, n_o), jnp.float32)
                     side_in[h, p, s] = jnp.zeros((n_a, LANES), jnp.float32)
     for s in both:
         @pl.when(jnp.logical_not(lat_has[s]))
         def _():
-            blank_rows = jnp.where(row == FIELDS - 1, 1.0, 0.0)
+            blank_rows = jnp.zeros((PACK, n_o), jnp.float32)
             for h in both:
                 for r in range(n_r):
                     row_in[h, s, r] = blank_rows
+                    more_in[h, s, r] = blank_rows + 1.0
                 for b in range(blocks_r):
                     for q in both:
                         corner_in[h, b, s, q] = jnp.zeros((1, LANES), jnp.float32)
                 for p in both:
-                    edge_in[h, s, p] = jnp.zeros((n_a, n_o), jnp.float32)
+                    edge_in[h, s, p] = blank_rows
             ids_near[s] = jnp.zeros(ids.shape, jnp.int32)
 
     def messages(h, b, early_part):
@@ -224,6 +229,10 @@
                 add(num.at[h, :, layer - 1], plane_num.at[h, 1 - p], *sems, device, rad_has[p])
                 if h == 0:
                     add(part.at[layer - 1], plane_d.at[1 - p], *sems, device, rad_has[p])
+        layers = pl.ds(b * UNROLL, UNROLL)
+        columns, rows, rows_at = (col_first, row_out, row_in) if early_part else (col_out, more_out, more_in)
+        lon_sems = (lon_send, lon_recv) if early_part else (late_lon_send, late_lon_recv)
+        lat_sems = (lat_send, lat_recv) if early_part else (late_lat_send, late_lat_recv)
         if early_part:
             for s in both:
                 for q in both:
@@ -232,22 +241,20 @@
                         far_send.at[s], far_recv.at[h, 1 - s],
                         {"lat": lat_to[s], "lon": lon_to[q]}, lat_has[s],
                     )
-            return table
         for q in both:
             add(
-                col_out.at[h, b], col_in.at[h, b, 1 - q], lon_send.at[0], lon_recv.at[h, b],
-                {"lon": lon_to[q]}, None,
+                columns.at[h, b], col_in.at[h, b, 0 if early_part else 1, 1 - q],
+                lon_sems[0].at[0], lon_sems[1].at[h, b], {"lon": lon_to[q]}, None,
             )
-        layers = pl.ds(b * UNROLL, UNROLL)
         for s in both:
             add(
-                row_out.at[h, s, layers], row_in.at[h, 1 - s, layers],
-                lat_send.at[s], lat_recv.at[h, b, 1 - s], {"lat": lat_to[s]}, lat_has[s],
+                rows.at[h, s, layers], rows_at.at[h, 1 - s, layers],
+                lat_sems[0].at[s], lat_sems[1].at[h, b, 1 - s], {"lat": lat_to[s]}, lat_has[s],
             )
         return table
 
     corner_rows = 2 * LANES // n_o
-    lat_rows = UNROLL * FIELDS
+    lat_rows = UNROLL * PACK
 
     def rad_rows(h):
         return (COMPS + (1 if h == 0 else 0)) * n_a
@@ -267,15 +274,23 @@
         for s in both:
             guarded(lat_has[s], functools.partial(await_rows, lat_recv.at[h, b, s], lat_rows))
 
+    def arrive_late(h, b):
+        await_rows(late_lon_recv.at[h, b], 2 * tile_rows)
+        for s in both:
+            guarded(lat_has[s], functools.partial(await_rows, late_lat_recv.at[h, b, s], lat_rows))
+
+    def arrive_planes(h):
+        for p in both:
+            guarded(rad_has[p], functools.partial(await_rows, rad_recv.at[h, p], rad_rows(h)))
+
     def arrive_far(h):
         for p in both:
-            guarded(rad_has[p], functools.partial(await_rows, rad_recv.at[h, p], rad_rows(h)))
             guarded(rad_has[p], functools.partial(await_rows, num_recv.at[h, p], num_rows(h)))
         for s in both:
             for p in both:
                 guarded(
                     all_of(rad_has[p], lat_has[s]),
-                    functools.partial(await_rows, edge_recv.at[h, s, p], FIELDS),
+                    functools.partial(await_rows, edge_recv.at[h, s, p], PACK),
                 )
             guarded(
                 lat_has[s],
@@ -289,11 +304,13 @@
             for s in both:
                 guarded(
                     all_of(rad_has[p], lat_has[s]),
-                    functools.partial(await_rows, edge_send.at[s, p], FIELDS, True),
+                    functools.partial(await_rows, edge_send.at[s, p], PACK, True),
                 )
         await_rows(lon_send.at[0], blocks_r * 2 * tile_rows, True)
-        for s in both:
-            guarded(lat_has[s], functools.partial(await_rows, lat_send.at[s], blocks_r * lat_rows, True))
+        await_rows(late_lon_send.at[0], blocks_r * 2 * tile_rows, True)
+        for s in both:
+            for sem in (lat_send, late_lat_send):
+                guarded(lat_has[s], functools.partial(await_rows, sem.at[s], blocks_r * lat_rows, True))
             guarded(lat_has[s], functools.partial(await_rows, far_send.at[s], blocks_r * corner_rows, True))
 
     def turn(x, shift, axis):
@@ -335,11 +352,11 @@
         low, high = (row_sum[t, s, r, 1 + c : 2 + c] for s in both)
         return edge_rows(low, high) + ends_of(col_sum[t, b], lane_at(1 + c, j))
 
-    def pack(h, r, k, tile, packed):
+    def pack(h, r, k, tile, packed, rows):
         for i in range(reps):
             piece = slice(i * LANES, (i + 1) * LANES)
-            row_out[h, 0, r, k : k + 1, piece] = tile[:1, piece]
-            row_out[h, 1, r, k : k + 1, piece] = tile[n_a - 1 :, piece]
+            rows[h, 0, r, k : k + 1, piece] = tile[:1, piece]
+            rows[h, 1, r, k : k + 1, piece] = tile[n_a - 1 :, piece]
         at = lane_at(k, r % UNROLL)
         two = jnp.where(lane < LANES // 2, tile[:, :LANES], tile[:, n_o - LANES :])
         hit = jnp.logical_and(field_of == k, layer_of == r % UNROLL)
@@ -354,7 +371,7 @@
             if h == 0:
                 tiles.append((0, eta[r + 1]))
             for k, tile in tiles:
-                packed = pack(h, r, k, tile, packed)
+                packed = pack(h, r, k, tile, packed, row_out)
                 for p, layer in ((0, 0), (1, n_r - 1)):
                     if r == layer:
                         for s in both:
@@ -367,7 +384,7 @@
 
     def prepare(h, b):
         t = 2 * h
-        packed = col_first[h, b]
+        packed = jnp.zeros((n_a, LANES), jnp.float32)
         for j in range(UNROLL):
             r = b * UNROLL + j
             if h == 0:
@@ -388,7 +405,7 @@
                 if r < n_r - 1:
                     d = d + harmonic(own, eta[r + 2])
                 part[r] = d
-                packed = pack(h, r, FIELDS - 1, d, packed)
+                packed = pack(h, r, 0, d, packed, more_out)
         for j in range(UNROLL):
             r = b * UNROLL + j
             for c in range(COMPS):
@@ -403,7 +420,7 @@
                 else:
                     total = f[c, r] + (near + radial(t, r, c, False))
                 num[h, c, r] = total
-                packed = pack(h, r, 1 + COMPS + c, total, packed)
+                packed = pack(h, r, 1 + c, total, packed, more_out)
         col_out[h, b] = packed
 
     def repeat_from(x, field, shifts):
@@ -414,19 +431,16 @@
     def repeat_first(x):
         return repeat_from(x, 0, range(COMPS + 1))
 
-    def repeat_last(x):
-        return repeat_from(x, FIELDS - 1, [1 + c - (FIELDS - 1) for c in range(COMPS)])
-
     def joined(from_west, from_east):
         at = even if from_west.shape[0] == n_a else even[:1]
         return jnp.where(at, turn(from_west, 1, 1), turn(from_east, -1, 1))
 
     def near_side(h, b):
         t = 2 * h
-        far = joined(col_in[h, b, 0], col_in[h, b, 1])
+        far = joined(col_in[h, b, 0, 0], col_in[h, b, 0, 1])
         col_far[h, b] = far
         if h == 0:
-            w = harmonic0(repeat_first(far), repeat_first(col_out[h, b]))
+            w = harmonic0(repeat_first(far), repeat_first(col_first[h, b]))
             col_w[b] = w
         else:
             w = col_w[b]
@@ -435,8 +449,8 @@
             for r in range(b * UNROLL, (b + 1) * UNROLL):
                 if h == 0:
                     w = harmonic(
-                        jnp.broadcast_to(row_in[h, s, r, :1], (n_a, n_o)),
-                        jnp.broadcast_to(row_out[h, s, r, :1], (n_a, n_o)),
+                        jnp.broadcast_to(row_in[h, s, r, :1], (PACK, n_o)),
+                        jnp.broadcast_to(row_out[h, s, r, :1], (PACK, n_o)),
                     )
                     row_w[s, r] = w
                 else:
@@ -450,13 +464,13 @@
                 r = b * UNROLL + j
                 far = row_in[h, s, r]
                 column = corner_t[h, b, pl.ds(lane_at(0, j), FIELDS, stride=2), :]
-                corner = ends_of(column, 2 * s + 1)
+                corner = ends_of(column, 2 * s + 1)[:PACK]
                 near = [p for p, layer in ((0, 0), (1, n_r - 1)) if r == layer]
                 w = row_w[s, r]
                 if h == 0:
-                    far_eta = jnp.broadcast_to(row_in[h, s, r, :1], (n_a, n_o))
+                    far_eta = jnp.broadcast_to(row_in[h, s, r, :1], (PACK, n_o))
                     wq = harmonic0(far_eta, corner[:1])
-                    d = row_in[h, s, r, FIELDS - 1 :] + (w + wq)
+                    d = more_in[h, s, r, :1] + (w + wq)
                     for p in near:
                         wp = harmonic0(far_eta, edge_in[h, s, p, :1])
                         row_p[s, p] = wp
@@ -466,7 +480,7 @@
                     row_g[s, r] = gain_far
                 else:
                     wq, gain_far = row_q[s, r], row_g[s, r]
-                total = turn(far, -COMPS, 0) + w * row_out[h, s, r] + wq * corner
+                total = more_in[h, s, r] + w * row_out[h, s, r] + wq * corner
                 for p in near:
                     total = total + row_p[s, p] * edge_in[h, s, p]
                 row_sum[t + 1, s, r] = w * ((1.0 - RELAX) * far + gain_far * total)
@@ -477,7 +491,8 @@
     def far_cols(h, b):
         t = 2 * h
         far = col_far[h, b]
-        own = col_out[h, b]
+        own = col_first[h, b]
+        more = joined(col_in[h, b, 1, 0], col_in[h, b, 1, 1])
         stacked = jnp.zeros((8, LANES), jnp.float32)
         spot = lax.broadcasted_iota(jnp.int32, (8, LANES), 0)
         for s in both:
@@ -490,7 +505,7 @@
         w = col_w[b]
         if h == 0:
             far_eta = repeat_first(far)
-            d = repeat_last(far) + w
+            d = repeat_first(more) + w
             for s in both:
                 wd = jnp.where(
                     row_thin == row_edge[s], harmonic0(far_eta, repeat_first(corners[s])), 0.0,
@@ -504,7 +519,7 @@
                 col_p[p] = wp
                 d = d + wp
             col_g[b] = RELAX / jnp.where(d > 0.0, d, 1.0)
-        total = turn(far, -2 * COMPS, 1) + w * own
+        total = more + w * own
         for s in both:
             total = total + col_d[b, s] * corners[s]
         for p in near_planes(b):
@@ -570,17 +585,39 @@
                 r, tile, total = whole_flux(t, b, c, j)
                 v[t + 1][c, r + 1] = (1.0 - RELAX) * tile + gain[r] * total
 
-    def residual(b):
+    def pair_rows(c, b, i):
+        return pl.ds((c * (n_r // 2) + b * (UNROLL // 2) + i) * n_a, n_a)
+
+    def begin_residual(b):
         t = SWEEPS
         for c in range(COMPS):
             for i in range(UNROLL // 2):
                 two = jnp.zeros((n_a, n_o), jnp.float32)
                 for j in (2 * i, 2 * i + 1):
-                    r, tile, total = whole_flux(t, b, c, j)
-                    two = two + (total - diag[r] * tile)
-                at = pl.ds((c * (n_r // 2) + b * (UNROLL // 2) + i) * n_a, n_a)
+                    r = b * UNROLL + j
+                    tile, near = interior(t, r, c)
+                    two = two + ((f[c, r] + near) + (radial(t, r, c, False) - diag[r] * tile))
                 for k in range(reps):
-                    pairs[k, at] = two[:, k * LANES : (k + 1) * LANES]
+                    pairs[k, pair_rows(c, b, i)] = two[:, k * LANES : (k + 1) * LANES]
+
+    def residual(b):
+        t = SWEEPS
+        for c in range(COMPS):
+            for i in range(UNROLL // 2):
+                rows = [
+                    sum(row_sum[t, s, b * UNROLL + j, 1 + c : 2 + c] for j in (2 * i, 2 * i + 1))
+                    for s in both
+                ]
+                more = edge_rows(*rows) + (
+                    ends_of(col_sum[t, b], lane_at(1 + c, 2 * i))
+                    + ends_of(col_sum[t, b], lane_at(1 + c, 2 * i + 1))
+                )
+                for r in (b * UNROLL + 2 * i, b * UNROLL + 2 * i + 1):
+                    if r in (0, n_r - 1):
+                        more = more + radial(t, r, c, True)
+                at = pair_rows(c, b, i)
+                for k in range(reps):
+                    pairs[k, at] = pairs[k, at] + more[:, k * LANES : (k + 1) * LANES]
 
     for b in reversed(range(blocks_r)):
         loaded(b)
@@ -589,6 +626,7 @@
     for b in reversed(range(blocks_r)):
         start(0, b, True)
     for b in reversed(range(blocks_r)):
+        loaded(b, True)
         phase(functools.partial(prepare, 0, b))
         start(0, b)
     load_ids.wait()
@@ -650,9 +688,13 @@
 
     onehots = [hot(ids[band : band + 1]) for band in range(bands)]
 
-    for k in range(1, waves):
-        wave_wait(k - 1)
-        wave_signal(k)
+    pending = list(range(1, waves))
+
+    def relay():
+        if pending:
+            k = pending.pop(0)
+            wave_wait(k - 1)
+            wave_signal(k)
 
     def s1_copy(step):
         return pltpu.make_async_remote_copy(
@@ -700,7 +742,7 @@
             shift = row_in[0, s, top, :1] * (moved[0] - moved[1])
             push = [shift[1 + c : 2 + c] for c in range(COMPS)]
             outer.append(cross(cos_tilt, (cos_tilt * cos_lon, cos_tilt * sin_lon, jnp.sin(tilt)), push))
-        moved = col_g[end] * col_w[end] * col_out[1, end]
+        moved = col_g[end] * col_w[end] * col_first[1, end]
         shift = repeat_first(col_far[0, end]) * (moved - turn(moved, 2 * FIELDS, 1))
         push = [ends_of(shift, lane_at(1 + c, UNROLL - 1)) for c in range(COMPS)]
         around = n_lon * n_o
@@ -750,6 +792,8 @@
                 s1_copy(step).start()
 
     def surface():
+        while pending:
+            relay()
         if waves:
             wave_wait(waves - 1)
         for i, (_, _, take) in enumerate(near_devices):
@@ -758,39 +802,49 @@
 
     def advance(b):
         phase(functools.partial(prepare, 1, b))
-        if b == end:
-            surface()
         start(1, b)
 
     def ready(b, done):
         return all(k in done for k in (b - 1, b, b + 1) if 0 <= k <= end)
 
     def sweep(h, order, finish, ship):
-        stepped, done, shipped = set(), set(), set()
+        done, shipped = set(), set()
 
         def near_part(b):
             near_side(h, b)
-            far_cols(h, b)
 
         def main_part(b):
             advance_face(h, b)
+
+        def far_part(b):
+            far_cols(h, b)
             far_rows(h, b)
 
-        for at, b in enumerate(order):
+        arrive_planes(h)
+        if h == 0:
+            for p in both:
+                pl.when(rad_has[p])(functools.partial(link_plane, p))
+        for b in order:
             arrive(h, b)
-            if at == 0:
-                arrive_far(h)
-                for p in both:
-                    if h == 0:
-                        pl.when(rad_has[p])(functools.partial(link_plane, p))
-                    pl.when(rad_has[p])(functools.partial(update_plane, h, p))
+            if b == order[0]:
+                relay()
             phase(functools.partial(near_part, b))
             phase(functools.partial(main_part, b))
-            stepped.add(b)
-            for k in order:
-                if k not in done and ready(k, stepped):
+        if h == 1:
+            for b in order:
+                phase(functools.partial(begin_residual, b))
+        arrive_far(h)
+        for p in both:
+            pl.when(rad_has[p])(functools.partial(update_plane, h, p))
+        for at, b in enumerate(order):
+            arrive_late(h, b)
+            phase(functools.partial(far_part, b))
+            for k in [b]:
+                if k not in done:
                     phase(functools.partial(finish, k))
                     done.add(k)
+                    if k == order[0]:
+                        relay()
                     if ship:
                         if k == end:
                             sent(0)
@@ -808,6 +862,7 @@
         advance(b)
 
     sweep(0, first_order, functools.partial(second_step, 1), ship_off)
+    surface()
 
     if not direct:
         @pl.when(is_top)
@@ -920,6 +975,7 @@
     coarse_rows = n_rad * (n_r // 2) * (n_a // 2)
     whole = (n_r, n_a, n_o)
     thin = (n_a, LANES)
+    flat = (PACK, n_o)
 
     def vmem(*shape):
         return pltpu.VMEM(shape, f32)
@@ -946,16 +1002,18 @@
             vmem(*whole),
             vmem(*whole),
             vmem(2, COMPS, *whole),
-            vmem(2, 2, *whole),
-            vmem(2, 2, *whole),
-            vmem(4, 2, *whole),
-            vmem(2, *whole),
-            vmem(2, *whole),
-            vmem(2, *whole),
-            vmem(2, 2, n_a, n_o),
+            vmem(2, 2, n_r, *flat),
+            vmem(2, 2, n_r, *flat),
+            vmem(2, 2, n_r, *flat),
+            vmem(2, 2, n_r, *flat),
+            vmem(4, 2, n_r, *flat),
+            vmem(2, n_r, *flat),
+            vmem(2, n_r, *flat),
+            vmem(2, n_r, *flat),
+            vmem(2, 2, *flat),
             vmem(2, chunks, *thin),
             vmem(2, chunks, *thin),
-            vmem(2, chunks, 2, *thin),
+            vmem(2, chunks, 2, 2, *thin),
             vmem(2, chunks, *thin),
             vmem(4, chunks, *thin),
             vmem(chunks, *thin),
@@ -970,8 +1028,8 @@
             vmem(2, chunks, 2, 1, LANES),
             vmem(2, chunks, 2, 2, 1, LANES),
             vmem(2, chunks, LANES, LANES),
-            vmem(2, 2, 2, n_a, n_o),
-            vmem(2, 2, 2, n_a, n_o),
+            vmem(2, 2, 2, *flat),
+            vmem(2, 2, 2, *flat),
             vmem(2, 2, 2, *thin),
             vmem(n_o // LANES, COMPS * (n_r // 2) * n_a, LANES),
             vmem(sources, 1, LANES),
@@ -979,12 +1037,16 @@
             vmem(2, 1, LANES),
             vmem(max(7 * UNROLL * n_a, chunks * (UNROLL * FIELDS + 8)), 1, n_o),
             vmem(max(group, sources, n_lat), 1, LANES),
-            dma((chunks + 1,)),
+            dma((2 * chunks + 1,)),
             dma((1,)),
             dma((2,)),
             dma((2,)),
             dma((2,)),
             dma((2, 2)),
+            dma((2, chunks)),
+            dma((2, chunks, 2)),
+            dma((1,)),
+            dma((2,)),
             dma((2, chunks)),
             dma((2, chunks, 2)),
             dma((2, 2)),

time: 20.5 us -> 19.3 us (0.941)
  Pallas kernels: 19.7 us -> 18.6 us
    pallas_call x1, Pallas kernels: 18.9 us -> 17.8 us  [on_device(): pl.pallas_call(functools.partial(kernel, sizes), out_shape=(pltpu.VMEM((C...]
where the time goes in v3:
time: 19.3 us; the launch traced here: 19.2 us
  Pallas kernels  18.6 us (96%)
  between operations  0.64 us (3%)
    pallas_call x1, Pallas kernels, on_device(): pl.pallas_call(functools.partial(kernel, sizes), out_shape=(pltpu.VMEM((C...  17.8 us
    pallas_call x1, Pallas kernels, on_device(): pl.pallas_call(write_out, out_shape=(jax.ShapeDtypeStruct(velocity.shape,...  0.8 us

profile of v3, /device:TPU:0, one launch (start us, length us, event | category | flops | bytes accessed | tf_op | source)
XLA Modules:
  0.0 19.2 jit_solution(11313631317836025239)
XLA Ops:
  0.6 17.8 %shard_map.67 = (f32[3,18,8,256]{3,2,1,0:T(8,128)S(1)}, f32[3,64,128]{2,1,0:T(8,128)S(1)}, f32[3,8,256]{2,1,0:T(8,128)S(1)}) custom-call(f32[3,16,8,256]{3,2,1,0:T(8,128)} %vel.1, f32[3,16,8,256]{3,2,1,0:T(8,128)} %forc.1, f32[16,8,256]{2,1,0:T(8,128)} %visc.1, s32[1,32]{1,0:T(1,128)} %ids_in.1), custom_call_target="tpu_custom_call" | custom-call | tf_op jit(solution)/shard_map/pallas_call | solution.py:983
  18.4 0.8 %shard_map.68 = (f32[3,16,8,256]{3,2,1,0:T(8,128)}, f32[3,64,128]{2,1,0:T(8,128)}, f32[3,8,256]{2,1,0:T(8,128)}) custom-call(f32[3,18,8,256]{3,2,1,0:T(8,128)S(1)} %get-tuple-element.9.last, f32[3,64,128]{2,1,0:T(8,128)S(1)} %get-tuple-element.10.coarse, f32[3,8,256]{2,1,0:T(8,128)S(1)} %get-tuple-element.11.plate), custom_call_target="tpu_custom_call" | custom-call | tf_op jit(solution)/shard_map/pallas_call | solution.py:1074

commit v4 on v3

--- a/solution.py
+++ b/solution.py
@@ -55,9 +55,10 @@
     corner_out, corner_in, corner_t, edge_out, edge_in, side_in,
     pairs, sums, lat_sums, stage_out, tally, tally_thin,
     load_sem, lon_send, lat_send, rad_send, num_send, edge_send, lon_recv, lat_recv, late_lon_send, late_lat_send, late_lon_recv, late_lat_recv, rad_recv, num_recv, edge_recv, far_send, far_recv,
-    ids_send, ids_recv, wave, s1_send, s1_recv, s2_send, s2_recv, g_send, g_recv,
+    ids_send, ids_recv, wave, misc,
 ):
     n_lat, n_lon, n_rad = sizes
+    g_send, g_recv, s2_send, s2_recv = misc.at[0:1], misc.at[1:2], misc.at[2], misc.at[3]
     n_r, n_a, n_o = visc.shape
     me_lat, me_lon, me_rad = (lax.axis_index(a) for a in ("lat", "lon", "rad"))
     lat_has = (me_lat > 0, me_lat < n_lat - 1)
@@ -67,6 +68,7 @@
     lon_to = (lax.rem(me_lon + n_lon - 1, n_lon), lax.rem(me_lon + 1, n_lon))
     is_top = me_rad == n_rad - 1
     direct = n_lat * n_lon * n_rad <= DIRECT
+    s1_send, s1_recv = (None, None) if direct else (misc.at[4], misc.at[5])
     v = [early.at[t] for t in range(SWEEPS)] + [last]
     blocks_r = n_r // UNROLL
     end = blocks_r - 1
@@ -113,7 +115,7 @@
         here_r = pl.ds(b * UNROLL, UNROLL)
         inner = pl.ds(1 + b * UNROLL, UNROLL)
         if rest:
-            return [pltpu.make_async_copy(forc.at[:, here_r], f.at[:, here_r], load_sem.at[blocks_r + b])]
+            return [pltpu.make_async_copy(forc.at[:, here_r], f.at[:, here_r], load_sem.at[blocks_r])]
         return [
             pltpu.make_async_copy(visc.at[here_r], eta.at[inner], load_sem.at[b]),
             pltpu.make_async_copy(vel.at[:, here_r], v[0].at[:, inner], load_sem.at[b]),
@@ -123,7 +125,7 @@
         for b in reversed(range(blocks_r)):
             for load in load_chunk(b, rest):
                 load.start()
-    load_ids = pltpu.make_async_copy(ids_in, ids, load_sem.at[2 * blocks_r])
+    load_ids = pltpu.make_async_copy(ids_in, ids, load_sem.at[blocks_r + 1])
     load_ids.start()
 
     def rows_of(ref):
@@ -143,10 +145,12 @@
         )
         copy.wait_send() if sending else copy.wait_recv()
 
-    def loaded(b, rest=False):
-        fields = COMPS if rest else COMPS + 1
-        some = tally.at[pl.ds(0, fields * UNROLL * n_a)]
-        pltpu.make_async_copy(some, some, load_sem.at[blocks_r + b if rest else b]).wait()
+    def loaded(b):
+        some = tally.at[pl.ds(0, (COMPS + 1) * UNROLL * n_a)]
+        pltpu.make_async_copy(some, some, load_sem.at[b]).wait()
+
+    def forcing_loaded():
+        pltpu.make_async_copy(f, f, load_sem.at[blocks_r]).wait()
 
     lane_wide = lax.broadcasted_iota(jnp.int32, (n_a, n_o), 1)
     lane = lax.broadcasted_iota(jnp.int32, (n_a, LANES), 1)
@@ -232,6 +236,7 @@
         layers = pl.ds(b * UNROLL, UNROLL)
         columns, rows, rows_at = (col_first, row_out, row_in) if early_part else (col_out, more_out, more_in)
         lon_sems = (lon_send, lon_recv) if early_part else (late_lon_send, late_lon_recv)
+        which = (h, b) if early_part else (h,)
         lat_sems = (lat_send, lat_recv) if early_part else (late_lat_send, late_lat_recv)
         if early_part:
             for s in both:
@@ -244,12 +249,12 @@
         for q in both:
             add(
                 columns.at[h, b], col_in.at[h, b, 0 if early_part else 1, 1 - q],
-                lon_sems[0].at[0], lon_sems[1].at[h, b], {"lon": lon_to[q]}, None,
+                lon_sems[0].at[0], lon_sems[1].at[*which], {"lon": lon_to[q]}, None,
             )
         for s in both:
             add(
                 rows.at[h, s, layers], rows_at.at[h, 1 - s, layers],
-                lat_sems[0].at[s], lat_sems[1].at[h, b, 1 - s], {"lat": lat_to[s]}, lat_has[s],
+                lat_sems[0].at[s], lat_sems[1].at[*which, 1 - s], {"lat": lat_to[s]}, lat_has[s],
             )
         return table
 
@@ -274,10 +279,12 @@
         for s in both:
             guarded(lat_has[s], functools.partial(await_rows, lat_recv.at[h, b, s], lat_rows))
 
-    def arrive_late(h, b):
-        await_rows(late_lon_recv.at[h, b], 2 * tile_rows)
-        for s in both:
-            guarded(lat_has[s], functools.partial(await_rows, late_lat_recv.at[h, b, s], lat_rows))
+    def arrive_late(h):
+        await_rows(late_lon_recv.at[h], blocks_r * 2 * tile_rows)
+        for s in both:
+            guarded(
+                lat_has[s], functools.partial(await_rows, late_lat_recv.at[h, s], blocks_r * lat_rows),
+            )
 
     def arrive_planes(h):
         for p in both:
@@ -573,17 +580,21 @@
                     total = total + radial(t, r, c, True)
                 v[t + 1][c, r + 1] = (1.0 - RELAX) * v[t][c, r + 1] + gain[r] * total
 
-    def whole_flux(t, b, c, j):
-        r = b * UNROLL + j
-        tile, near = interior(t, r, c)
-        total = (f[c, r] + near) + (radial(t, r, c, None) + seams(t, b, j, c))
-        return r, tile, total
-
-    def second_step(t, b):
+    def begin_second(b):
         for c in range(COMPS):
             for j in range(UNROLL):
-                r, tile, total = whole_flux(t, b, c, j)
-                v[t + 1][c, r + 1] = (1.0 - RELAX) * tile + gain[r] * total
+                r = b * UNROLL + j
+                _, near = interior(1, r, c)
+                num[1, c, r] = f[c, r] + (near + radial(1, r, c, False))
+
+    def second_step(b):
+        for c in range(COMPS):
+            for j in range(UNROLL):
+                r = b * UNROLL + j
+                total = num[1, c, r] + seams(1, b, j, c)
+                if r in (0, n_r - 1):
+                    total = total + radial(1, r, c, True)
+                v[2][c, r + 1] = (1.0 - RELAX) * v[1][c, r + 1] + gain[r] * total
 
     def pair_rows(c, b, i):
         return pl.ds((c * (n_r // 2) + b * (UNROLL // 2) + i) * n_a, n_a)
@@ -625,8 +636,8 @@
     pl.semaphore_wait(barrier, expected)
     for b in reversed(range(blocks_r)):
         start(0, b, True)
+    forcing_loaded()
     for b in reversed(range(blocks_r)):
-        loaded(b, True)
         phase(functools.partial(prepare, 0, b))
         start(0, b)
     load_ids.wait()
@@ -698,7 +709,7 @@
 
     def s1_copy(step):
         return pltpu.make_async_remote_copy(
-            stage_out.at[0], lat_sums.at[me_lat], s1_send.at[0], s1_recv.at[0],
+            stage_out.at[0], lat_sums.at[me_lat], s1_send, s1_recv,
             device_id={"lat": lax.rem(me_lat + step, n_lat)}, device_id_type=MESH,
         )
 
@@ -714,7 +725,7 @@
         if direct:
             device["lat"] = lax.rem(me_lat + step // plane, n_lat)
         return pltpu.make_async_remote_copy(
-            stage_out.at[1], sums.at[here], s2_send.at[0], s2_recv.at[0],
+            stage_out.at[1], sums.at[here], s2_send, s2_recv,
             device_id=device, device_id_type=MESH,
         )
 
@@ -830,14 +841,13 @@
                 relay()
             phase(functools.partial(near_part, b))
             phase(functools.partial(main_part, b))
-        if h == 1:
-            for b in order:
-                phase(functools.partial(begin_residual, b))
+        for b in order:
+            phase(functools.partial((begin_second, begin_residual)[h], b))
         arrive_far(h)
         for p in both:
             pl.when(rad_has[p])(functools.partial(update_plane, h, p))
+        arrive_late(h)
         for at, b in enumerate(order):
-            arrive_late(h, b)
             phase(functools.partial(far_part, b))
             for k in [b]:
                 if k not in done:
@@ -861,13 +871,13 @@
     def ship_off(b):
         advance(b)
 
-    sweep(0, first_order, functools.partial(second_step, 1), ship_off)
+    sweep(0, first_order, second_step, ship_off)
     surface()
 
     if not direct:
         @pl.when(is_top)
         def _():
-            await_thin(s1_recv.at[0], n_lat - 1)
+            await_thin(s1_recv, n_lat - 1)
             total = lat_sums[0]
             for i in range(1, n_lat):
                 total = total + lat_sums[i]
@@ -899,7 +909,7 @@
 
     def g_copy(step):
         return pltpu.make_async_remote_copy(
-            coarse.at[:, spot], coarse.at[:, spot], g_send.at[step - 1], g_recv.at[me_rad],
+            coarse.at[:, spot], coarse.at[:, spot], g_send.at[0], g_recv.at[0],
             device_id={"rad": lax.rem(me_rad + step, n_rad)}, device_id_type=MESH,
         )
 
@@ -907,8 +917,8 @@
         g_copy(step).start()
 
     sources = n_lat * n_lon if direct else n_lon
-    pl.when(is_top)(functools.partial(await_thin, s2_recv.at[0], sources - 1))
-    pl.when(jnp.logical_not(is_top))(functools.partial(await_thin, s2_recv.at[0], sources))
+    pl.when(is_top)(functools.partial(await_thin, s2_recv, sources - 1))
+    pl.when(jnp.logical_not(is_top))(functools.partial(await_thin, s2_recv, sources))
     terms = [sums[i] for i in range(sources)]
     while len(terms) > 1:
         terms = [terms[i] + terms[i + 1] if i + 1 < len(terms) else terms[i] for i in range(0, len(terms), 2)]
@@ -935,17 +945,12 @@
     @pl.when(is_top)
     def _():
         if not direct:
-            await_thin(s1_send.at[0], n_lat - 1, True)
-        await_thin(s2_send.at[0], group - 1, True)
-
-    for step in range(1, n_rad):
-        source = lax.rem(me_rad + step, n_rad)
-        region = coarse.at[:, pl.ds(pl.multiple_of(source * mine, mine), mine)]
-        pltpu.make_async_remote_copy(
-            region, region, g_send.at[0], g_recv.at[source],
-            device_id={"rad": source}, device_id_type=MESH,
-        ).wait_recv()
-        g_copy(step).wait_send()
+            await_thin(s1_send, n_lat - 1, True)
+        await_thin(s2_send, group - 1, True)
+
+    gathered = (n_rad - 1) * COMPS * mine // 2
+    await_rows(g_recv.at[0], gathered)
+    await_rows(g_send.at[0], gathered, True)
 
 
 def write_out(last, coarse, plate, new_v_out, coarse_out, plate_out, sem):
@@ -1037,7 +1042,7 @@
             vmem(2, 1, LANES),
             vmem(max(7 * UNROLL * n_a, chunks * (UNROLL * FIELDS + 8)), 1, n_o),
             vmem(max(group, sources, n_lat), 1, LANES),
-            dma((2 * chunks + 1,)),
+            dma((chunks + 2,)),
             dma((1,)),
             dma((2,)),
             dma((2,)),
@@ -1047,8 +1052,8 @@
             dma((2, chunks, 2)),
             dma((1,)),
             dma((2,)),
-            dma((2, chunks)),
-            dma((2, chunks, 2)),
+            dma((2,)),
+            dma((2, 2)),
             dma((2, 2)),
             dma((2, 2)),
             dma((2, 2, 2)),
@@ -1057,12 +1062,7 @@
             dma((4,)),
             dma((4,)),
             pltpu.SemaphoreType.REGULAR((n_lat - 1 if direct else 1, 2)),
-            dma((1,)),
-            dma((1,)),
-            dma((1,)),
-            dma((1,)),
-            dma((n_rad,)),
-            dma((n_rad,)),
+            dma((4 if direct else 6,)),
         ],
         compiler_params=pltpu.CompilerParams(
             collective_id=0, has_side_effects=True, vmem_limit_bytes=32 * 2**20

time: 19.3 us -> 19 us (0.984)
  Pallas kernels: 18.6 us -> 18.2 us
    pallas_call x1, Pallas kernels: 17.8 us -> 17.4 us  [on_device(): pl.pallas_call(functools.partial(kernel, sizes), out_shape=(pltpu.VMEM((C...]
where the time goes in v4:
time: 19 us; the launch traced here: 18.9 us
  Pallas kernels  18.2 us (96%)
  between operations  0.64 us (3%)
    pallas_call x1, Pallas kernels, on_device(): pl.pallas_call(functools.partial(kernel, sizes), out_shape=(pltpu.VMEM((C...  17.4 us
    pallas_call x1, Pallas kernels, on_device(): pl.pallas_call(write_out, out_shape=(jax.ShapeDtypeStruct(velocity.shape,...  0.8 us

profile of v4, /device:TPU:0, one launch (start us, length us, event | category | flops | bytes accessed | tf_op | source)
XLA Modules:
  0.0 18.9 jit_solution(16706639556922059036)
XLA Ops:
  0.6 17.4 %shard_map.67 = (f32[3,18,8,256]{3,2,1,0:T(8,128)S(1)}, f32[3,64,128]{2,1,0:T(8,128)S(1)}, f32[3,8,256]{2,1,0:T(8,128)S(1)}) custom-call(f32[3,16,8,256]{3,2,1,0:T(8,128)} %vel.1, f32[3,16,8,256]{3,2,1,0:T(8,128)} %forc.1, f32[16,8,256]{2,1,0:T(8,128)} %visc.1, s32[1,32]{1,0:T(1,128)} %ids_in.1), custom_call_target="tpu_custom_call" | custom-call | tf_op jit(solution)/shard_map/pallas_call | solution.py:988
  18.1 0.8 %shard_map.68 = (f32[3,16,8,256]{3,2,1,0:T(8,128)}, f32[3,64,128]{2,1,0:T(8,128)}, f32[3,8,256]{2,1,0:T(8,128)}) custom-call(f32[3,18,8,256]{3,2,1,0:T(8,128)S(1)} %get-tuple-element.9.last, f32[3,64,128]{2,1,0:T(8,128)S(1)} %get-tuple-element.10.coarse, f32[3,8,256]{2,1,0:T(8,128)S(1)} %get-tuple-element.11.plate), custom_call_target="tpu_custom_call" | custom-call | tf_op jit(solution)/shard_map/pallas_call | solution.py:1074

commit v5 on v4

--- a/solution.py
+++ b/solution.py
@@ -54,7 +54,7 @@
     plane_num, plane_d, plane_g, plane_l, plane_q,
     corner_out, corner_in, corner_t, edge_out, edge_in, side_in,
     pairs, sums, lat_sums, stage_out, tally, tally_thin,
-    load_sem, lon_send, lat_send, rad_send, num_send, edge_send, lon_recv, lat_recv, late_lon_send, late_lat_send, late_lon_recv, late_lat_recv, rad_recv, num_recv, edge_recv, far_send, far_recv,
+    load_sem, lon_send, lat_send, rad_send, edge_send, lon_recv, lat_recv, late_lon_recv, late_lat_recv, rad_recv, num_recv, edge_recv, far_recv,
     ids_send, ids_recv, wave, misc,
 ):
     n_lat, n_lon, n_rad = sizes
@@ -216,7 +216,7 @@
                 add(v[t].at[:, layer], v[t].at[:, slot], *sems, device, rad_has[p])
                 if h == 0:
                     add(eta.at[layer], eta.at[slot], *sems, device, rad_has[p])
-            sems = (num_send.at[p], num_recv.at[h, 1 - p])
+            sems = (rad_send.at[p], num_recv.at[h, 1 - p])
             if early_part:
                 for q in both:
                     add(
@@ -235,15 +235,15 @@
                     add(part.at[layer - 1], plane_d.at[1 - p], *sems, device, rad_has[p])
         layers = pl.ds(b * UNROLL, UNROLL)
         columns, rows, rows_at = (col_first, row_out, row_in) if early_part else (col_out, more_out, more_in)
-        lon_sems = (lon_send, lon_recv) if early_part else (late_lon_send, late_lon_recv)
+        lon_sems = (lon_send, lon_recv) if early_part else (lon_send, late_lon_recv)
         which = (h, b) if early_part else (h,)
-        lat_sems = (lat_send, lat_recv) if early_part else (late_lat_send, late_lat_recv)
+        lat_sems = (lat_send, lat_recv) if early_part else (lat_send, late_lat_recv)
         if early_part:
             for s in both:
                 for q in both:
                     add(
                         corner_out.at[h, b, s], corner_in.at[h, b, 1 - s, 1 - q],
-                        far_send.at[s], far_recv.at[h, 1 - s],
+                        lat_send.at[s], far_recv.at[h, 1 - s],
                         {"lat": lat_to[s], "lon": lon_to[q]}, lat_has[s],
                     )
         for q in both:
@@ -306,19 +306,23 @@
 
     def sent(h):
         for p in both:
-            guarded(rad_has[p], functools.partial(await_rows, rad_send.at[p], rad_rows(h), True))
-            guarded(rad_has[p], functools.partial(await_rows, num_send.at[p], num_rows(h), True))
+            guarded(
+                rad_has[p],
+                functools.partial(await_rows, rad_send.at[p], rad_rows(h) + num_rows(h), True),
+            )
             for s in both:
                 guarded(
                     all_of(rad_has[p], lat_has[s]),
                     functools.partial(await_rows, edge_send.at[s, p], PACK, True),
                 )
-        await_rows(lon_send.at[0], blocks_r * 2 * tile_rows, True)
-        await_rows(late_lon_send.at[0], blocks_r * 2 * tile_rows, True)
-        for s in both:
-            for sem in (lat_send, late_lat_send):
-                guarded(lat_has[s], functools.partial(await_rows, sem.at[s], blocks_r * lat_rows, True))
-            guarded(lat_has[s], functools.partial(await_rows, far_send.at[s], blocks_r * corner_rows, True))
+        await_rows(lon_send.at[0], 2 * blocks_r * 2 * tile_rows, True)
+        for s in both:
+            guarded(
+                lat_has[s],
+                functools.partial(
+                    await_rows, lat_send.at[s], blocks_r * (2 * lat_rows + corner_rows), True,
+                ),
+            )
 
     def turn(x, shift, axis):
         shift = shift % x.shape[axis]
@@ -839,8 +843,11 @@
             arrive(h, b)
             if b == order[0]:
                 relay()
-            phase(functools.partial(near_part, b))
-            phase(functools.partial(main_part, b))
+            def both_parts(b=b):
+                near_part(b)
+                main_part(b)
+
+            phase(both_parts)
         for b in order:
             phase(functools.partial((begin_second, begin_residual)[h], b))
         arrive_far(h)
@@ -1046,18 +1053,14 @@
             dma((1,)),
             dma((2,)),
             dma((2,)),
-            dma((2,)),
             dma((2, 2)),
             dma((2, chunks)),
             dma((2, chunks, 2)),
-            dma((1,)),
-            dma((2,)),
             dma((2,)),
             dma((2, 2)),
             dma((2, 2)),
             dma((2, 2)),
             dma((2, 2, 2)),
-            dma((2,)),
             dma((2, 2)),
             dma((4,)),
             dma((4,)),

time: 19 us -> 19 us (level)
  no operation moved by 1% of the time
where the time goes in v5:
time: 19 us; the launch traced here: 18.8 us
  Pallas kernels  18.2 us (96%)
  between operations  0.64 us (3%)
    pallas_call x1, Pallas kernels, on_device(): pl.pallas_call(functools.partial(kernel, sizes), out_shape=(pltpu.VMEM((C...  17.4 us
    pallas_call x1, Pallas kernels, on_device(): pl.pallas_call(write_out, out_shape=(jax.ShapeDtypeStruct(velocity.shape,...  0.8 us

profile of v5, /device:TPU:0, one launch (start us, length us, event | category | flops | bytes accessed | tf_op | source)
XLA Modules:
  0.0 18.8 jit_solution(9474553382514709393)
XLA Ops:
  0.6 17.4 %shard_map.67 = (f32[3,18,8,256]{3,2,1,0:T(8,128)S(1)}, f32[3,64,128]{2,1,0:T(8,128)S(1)}, f32[3,8,256]{2,1,0:T(8,128)S(1)}) custom-call(f32[3,16,8,256]{3,2,1,0:T(8,128)} %vel.1, f32[3,16,8,256]{3,2,1,0:T(8,128)} %forc.1, f32[16,8,256]{2,1,0:T(8,128)} %visc.1, s32[1,32]{1,0:T(1,128)} %ids_in.1), custom_call_target="tpu_custom_call" | custom-call | tf_op jit(solution)/shard_map/pallas_call | solution.py:995
  18.0 0.8 %shard_map.68 = (f32[3,16,8,256]{3,2,1,0:T(8,128)}, f32[3,64,128]{2,1,0:T(8,128)}, f32[3,8,256]{2,1,0:T(8,128)}) custom-call(f32[3,18,8,256]{3,2,1,0:T(8,128)S(1)} %get-tuple-element.9.last, f32[3,64,128]{2,1,0:T(8,128)S(1)} %get-tuple-element.10.coarse, f32[3,8,256]{2,1,0:T(8,128)S(1)} %get-tuple-element.11.plate), custom_call_target="tpu_custom_call" | custom-call | tf_op jit(solution)/shard_map/pallas_call | solution.py:1077
